TPU v7x, 512 devices: a whole 4x4x16 slice. The times are simulated.
512 devices in a mesh: seq: 128 (over z, y, core), tp: 4 (over x).
Axes of the slice: x: 4, y: 4, z: 16, core: 2. Of those that a mesh axis runs over, the one named last changes fastest.
Arguments:
- query_states: bfloat16 [8192, 4096], P('seq', 'tp'), may hold values from -384 to 384
- key_states: bfloat16 [8192, 4096], P('seq', 'tp'), may hold values from -12 to 12
- value_states: bfloat16 [8192, 4096], P('seq', 'tp'), may hold values from -6 to 6
- residual: bfloat16 [8192, 4096], P('seq', 'tp'), may hold values from -3 to 3
- segment_ids: int32 [8192], replicated, may hold values from 0 to 7, never falling along the last dimension, each value on 1 to 4096 neighbouring positions
- positions: int32 [2, 8192], P(None, 'seq'), may hold values from 0 to 63
- out_weight: bfloat16 [4096, 4096], P('tp', 'seq'), may hold values from -0.375 to 0.375
- layer_scale: float32 [4096], P('tp'), may hold values from 0.5 to 2
Outputs:
- encoded: bfloat16 [8192, 4096], P('seq', 'tp')
Inputs may be any that keep to these rules, and one draw needn't show every extreme that they name: `segment_ids`: the ids never fall along the row, and each id covers one run of at most 4096 positions.
All inputs are finite; a program needn't handle non-finite values.
Results may differ from a plain program's by a relative error of at most 0.0072.
Values may be sent and summed in bfloat16 or wider, within the bound.
A program may use at most 128 MiB of HBM per device.

v0:
```python
import jax
import jax.numpy as jnp
from jax import lax
from jax.sharding import PartitionSpec as P

DH = 128


masked_score = -1e30


def rotary(states, positions):
    quarter = DH // 4
    frequency = 100.0 ** (-jnp.arange(quarter, dtype=jnp.float32) / quarter)
    angles = positions.astype(jnp.float32)[:, :, None] * frequency
    angles = jnp.moveaxis(angles, 0, 1)
    cosine = jnp.cos(angles)[:, None, :, None, :]
    sine_table = jnp.sin(angles)[:, None, :, None, :]
    local_span, feature_width = states.shape
    shaped = states.reshape(local_span, feature_width // DH, 2, 2, quarter)
    partner = jnp.flip(shaped, axis=3)
    signed = jnp.array([-1.0, 1.0], jnp.float32)[:, None]
    rotated = shaped * cosine + partner * sine_table * signed
    return rotated.reshape(local_span, feature_width)


def attend_block(query_block, query_segments, key_item, value_item, segment_row):
    scores = jnp.dot(query_block, key_item.T, preferred_element_type=jnp.float32) * DH ** (-0.5)
    allowed = query_segments[:, None] == segment_row[None, :]
    scores = jnp.where(allowed, scores, masked_score)
    row_peak = jnp.max(scores, axis=1, keepdims=True)
    exponent = jnp.exp(scores - row_peak)
    row_total = jnp.sum(exponent, axis=1, keepdims=True)
    weights = exponent.astype(jnp.bfloat16)
    weighted = jnp.dot(weights, value_item, preferred_element_type=jnp.float32)
    return (weighted / row_total).astype(jnp.bfloat16)


def local(
    query_states,
    key_states,
    value_states,
    residual,
    segment_ids,
    positions,
    out_weight,
    layer_scale,
):
    local_span, feature_width = query_states.shape
    head_count = feature_width // DH
    seq_count = lax.axis_size("seq")
    query_parts = seq_count // head_count
    slice_len = local_span // query_parts
    rotated_q = rotary(query_states.astype(jnp.float32), positions).astype(jnp.bfloat16)
    rotated_k = rotary(key_states.astype(jnp.float32), positions).astype(jnp.bfloat16)
    part_here = lax.axis_index("seq") % query_parts
    query_send = rotated_q.reshape(query_parts, slice_len, head_count, DH).transpose(2, 0, 1, 3)
    query_send = query_send.reshape(seq_count, slice_len, DH)

    def spread(states):
        by_head = states.reshape(local_span, head_count, DH).transpose(1, 0, 2)
        widened = jnp.broadcast_to(by_head[:, None], (head_count, query_parts, local_span, DH))
        return widened.reshape(seq_count, local_span, DH)

    query_got, key_got, value_got = (
        lax.all_to_all(query_send, "seq", split_axis=0, concat_axis=1, tiled=True),
        lax.all_to_all(spread(rotated_k), "seq", split_axis=0, concat_axis=1, tiled=True),
        lax.all_to_all(spread(value_states), "seq", split_axis=0, concat_axis=1, tiled=True),
    )
    query_item = query_got[0]
    key_item = key_got[0]
    value_item = value_got[0]
    segment_grid = segment_ids.reshape(seq_count, query_parts, slice_len)
    query_segment_row = lax.dynamic_index_in_dim(
        segment_grid, part_here, 1, keepdims=False
    ).reshape(-1)
    length = query_item.shape[0]
    block_rows = min(512, length)

    def per_block(block_index):
        return attend_block(query_item, query_segment_row, key_item, value_item, segment_ids)

    attended = lax.map(per_block, jnp.arange(length // block_rows, dtype=jnp.int32))
    attended = attended.reshape(seq_count, slice_len, DH)
    returned = lax.all_to_all(attended, "seq", split_axis=0, concat_axis=0, tiled=True)
    flat_tokens = returned.reshape(head_count, query_parts, slice_len, DH).transpose(1, 2, 0, 3)
    flat_tokens = flat_tokens.reshape(local_span, feature_width)
    partial_value = jnp.dot(
        flat_tokens,
        lax.all_gather(out_weight, "seq", axis=1, tiled=True),
        preferred_element_type=jnp.float32,
    )
    summed = lax.psum_scatter(partial_value, "tp", scatter_dimension=1, tiled=True)
    encoded = residual.astype(jnp.float32) + layer_scale * summed
    return encoded.astype(jnp.bfloat16)


def solution(mesh):
    in_specs = (
        P("seq", "tp"),
        P("seq", "tp"),
        P("seq", "tp"),
        P("seq", "tp"),
        P(),
        P(None, "seq"),
        P("tp", "seq"),
        P("tp"),
    )
    out_specs = P("seq", "tp")
    return jax.shard_map(local, mesh=mesh, in_specs=in_specs, out_specs=out_specs, check_vma=False)
```

profile of v0, /device:TPU:1, one launch (start us, length us, event | category | flops | bytes accessed | tf_op | source)
XLA Modules:
  0.0 358.0 jit_solution(14117068359550184412)
XLA Ops:
  6.5 0.7 convert_bitcast_fusion
  7.2 1.1 copy.29
  8.4 1.1 copy.33
  9.7 0.9 add_convert_fusion
  10.7 0.5 copy.30
  11.6 0.8 copy.32
  12.3 20.6 %all-to-all-start = ((bf16[128,4,128]{2,1,0:T(4,128)(2,1)}), bf16[128,4,128]{2,1,0:T(4,128)(2,1)S(1)}, u32[]{:S(2)}, u32[]{:S(2)}) async-start(bf16[128,4,128]{2,1,0:T(4,128)(2,1)} %copy.32), calls=%async_computation | async-start | bytes 262144 | tf_op jit(solution)/shard_map/all_to_all | solution.py:66
  33.0 15.9 %all-to-all-done = bf16[128,4,128]{2,1,0:T(4,128)(2,1)S(1)} async-done(((bf16[128,4,128]{2,1,0:T(4,128)(2,1)}), bf16[128,4,128]{2,1,0:T(4,128)(2,1)S(1)}, u32[]{:S(2)}, u32[]{:S(2)}) %all-to-all-start) | async-done | bytes 131104 | tf_op jit(solution)/shard_map/all_to_all | solution.py:66
  48.9 1.9 broadcast_in_dim.13
  50.8 7.2 %all-to-all-start.1 = ((bf16[128,64,128]{2,1,0:T(8,128)(2,1)}), bf16[128,64,128]{2,1,0:T(8,128)(2,1)S(1)}, u32[]{:S(2)}, u32[]{:S(2)}) async-start(bf16[128,64,128]{2,1,0:T(8,128)(2,1)} %bitcast.10), calls=%async_computation.1 | async-start | bytes 4194304 | tf_op jit(solution)/shard_map/all_to_all | solution.py:67
  58.0 0.7 all-gather.2.cloned.1.call-update
  58.7 0.9 copy.38
  59.7 100.4 %all-to-all-done.1 = bf16[128,64,128]{2,1,0:T(8,128)(2,1)S(1)} async-done(((bf16[128,64,128]{2,1,0:T(8,128)(2,1)}), bf16[128,64,128]{2,1,0:T(8,128)(2,1)S(1)}, u32[]{:S(2)}, u32[]{:S(2)}) %all-to-all-start.1) | async-done | bytes 2097184 | tf_op jit(solution)/shard_map/all_to_all | solution.py:67
  160.1 2.0 broadcast_in_dim.15
  162.0 10.2 %all-to-all-start.2 = ((bf16[128,64,128]{2,1,0:T(8,128)(2,1)}), bf16[128,64,128]{2,1,0:T(8,128)(2,1)S(1)}, u32[]{:S(2)}, u32[]{:S(2)}) async-start(bf16[128,64,128]{2,1,0:T(8,128)(2,1)} %bitcast.13), calls=%async_computation.2 | async-start | bytes 4194304 | tf_op jit(solution)/shard_map/all_to_all | solution.py:68
  172.5 1.1 reshape.80
  173.9 8.8 %fusion.14 = (f32[512]{0:T(512)S(1)}, f32[512,8192]{1,0:T(8,128)}) fusion(bf16[512,128]{1,0:T(8,128)(2,1)S(1)} %bitcast.45, bf16[8192,128]{1,0:T(8,128)(2,1)} %bitcast.34, s32[8192]{0:T(1024)S(1)} %copy-done.2, s32[512]{0:T(512)S(1)} %eq.24), kind=kOutput, calls=%fused_computation.19 | convolution fusion | flops 1090518528 | bytes 19042304 | tf_op jit(solution)/shard_map/while/body/eval_jaxpr/dot_general | solution.py:28
  182.7 8.2 %fusion = f32[512]{0:T(512)S(1)} fusion(f32[512,8192]{1,0:T(8,128)} %get-tuple-element.30, f32[512]{0:T(512)S(1)} %get-tuple-element.28), kind=kLoop, calls=%fused_computation.2 | loop fusion | flops 8388096 | bytes 16781312 | tf_op jit(solution)/shard_map/while/body/eval_jaxpr/reduce_sum | solution.py:33
  190.9 96.1 %all-to-all-done.2 = bf16[128,64,128]{2,1,0:T(8,128)(2,1)S(1)} async-done(((bf16[128,64,128]{2,1,0:T(8,128)(2,1)}), bf16[128,64,128]{2,1,0:T(8,128)(2,1)S(1)}, u32[]{:S(2)}, u32[]{:S(2)}) %all-to-all-start.2) | async-done | bytes 2097184 | tf_op jit(solution)/shard_map/all_to_all | solution.py:68
  287.0 8.2 %fusion.8 = bf16[512,128]{1,0:T(8,128)(2,1)S(1)} fusion(bf16[8192,128]{1,0:T(8,128)(2,1)S(1)} %bitcast.33, f32[512,8192]{1,0:T(8,128)} %get-tuple-element.30, f32[512]{0:T(512)S(1)} %get-tuple-element.28, f32[512]{0:T(512)S(1)} %fusion), kind=kOutput, calls=%fused_computation.7 | convolution fusion | flops 1082261504 | bytes 19009536 | tf_op jit(solution)/shard_map/while/body/eval_jaxpr/dot_general | solution.py:35
  295.1 26.4 %all_to_all.32 = bf16[128,4,128]{2,1,0:T(4,128)(2,1)S(1)} all-to-all(bf16[128,4,128]{2,1,0:T(4,128)(2,1)S(1)} %bitcast.39), channel_id=1, replica_groups=mesh['seq'=128,'tp'=4] {'seq'}, dimensions={0} | all-to-all | bytes 262144 | tf_op jit(solution)/shard_map/all_to_all | solution.py:85
  321.6 7.0 %fusion.11 = f32[64,4096]{1,0:T(8,128)} fusion(bf16[1024,4096]{0,1:T(8,128)(2,1)} %all-gather.2.cloned.1.call-done, bf16[8,8,8,128]{3,2,1,0:T(8,128)(2,1)S(1)} %bitcast.38), kind=kOutput, calls=%fused_computation.11 | convolution fusion | flops 536870912 | bytes 9568256 | tf_op jit(solution)/shard_map/dot_general | solution.py:88
  328.7 20.8 %reduce-scatter.2.cloned.1.call-done = f32[64,1024]{1,0:T(8,128)} async-done(((f32[64,4096]{1,0:T(8,128)}), f32[64,1024]{1,0:T(8,128)}) %reduce-scatter.2.cloned.1.call-update) | async-done | bytes 262160 | tf_op jit(solution)/shard_map/reduce_scatter | solution.py:93
  349.5 1.6 add_convert_fusion.2
  (24 shorter events, 1.5 us)
Async XLA Ops:
  6.5 166.0 %copy-start.2 = (s32[8192]{0:T(1024)S(1)}, s32[8192]{0:T(1024)}, u32[]{:S(2)}) copy-start(s32[8192]{0:T(1024)} %param.14) | copy-start | bytes 98308
  12.3 36.6 %all-to-all-start = ((bf16[128,4,128]{2,1,0:T(4,128)(2,1)}), bf16[128,4,128]{2,1,0:T(4,128)(2,1)S(1)}, u32[]{:S(2)}, u32[]{:S(2)}) async-start(bf16[128,4,128]{2,1,0:T(4,128)(2,1)} %copy.32), calls=%async_computation | async-start | bytes 262144 | tf_op jit(solution)/shard_map/all_to_all | solution.py:66
  50.8 109.2 %all-to-all-start.1 = ((bf16[128,64,128]{2,1,0:T(8,128)(2,1)}), bf16[128,64,128]{2,1,0:T(8,128)(2,1)S(1)}, u32[]{:S(2)}, u32[]{:S(2)}) async-start(bf16[128,64,128]{2,1,0:T(8,128)(2,1)} %bitcast.10), calls=%async_computation.1 | async-start | bytes 4194304 | tf_op jit(solution)/shard_map/all_to_all | solution.py:67
  58.0 263.6 %all-gather.2.cloned.1.call-start = ((), (), s32[]{:S(2)}) async-start(), calls=%async_computation.5 | async-start | bytes 8454144 | tf_op jit(solution)/shard_map/all_gather | solution.py:90
  160.1 2.0 copy-start
  162.0 124.9 %all-to-all-start.2 = ((bf16[128,64,128]{2,1,0:T(8,128)(2,1)}), bf16[128,64,128]{2,1,0:T(8,128)(2,1)S(1)}, u32[]{:S(2)}, u32[]{:S(2)}) async-start(bf16[128,64,128]{2,1,0:T(8,128)(2,1)} %bitcast.13), calls=%async_computation.2 | async-start | bytes 4194304 | tf_op jit(solution)/shard_map/all_to_all | solution.py:68
  172.2 177.2 %reduce-scatter.2.cloned.1.call-start = ((), (), s32[]{:S(2)}) async-start(), calls=%async_computation.6 | async-start | bytes 1310720 | tf_op jit(solution)/shard_map/reduce_scatter | solution.py:93
  190.9 158.6 %copy-start.1 = (bf16[64,1024]{1,0:T(8,128)(2,1)S(1)}, bf16[64,1024]{1,0:T(8,128)(2,1)}, u32[]{:S(2)}) copy-start(bf16[64,1024]{1,0:T(8,128)(2,1)} %param.13) | copy-start | bytes 393220
  190.9 158.6 %copy-start.3 = (f32[1024]{0:T(1024)S(1)}, f32[1024]{0:T(1024)}, u32[]{:S(2)}) copy-start(f32[1024]{0:T(1024)} %param.17) | copy-start | bytes 12292
Sparse Core Ops, SparseCore 0:
  62.0 216.8 all-gather.1
  328.8 20.6 reduce-scatter.1
where the time goes:
time: 360 us; the launch traced here: 358 us
  waiting for transfers between devices  234 us (65%)
  starting transfers between devices  38.2 us (11%)
  blocking collectives  26.4 us (7%)
  matrix products  24 us (7%)
  between operations  13.6 us (4%)
  other arithmetic  11.7 us (3%)
  local copies, waits for them, and re-layouts  10.2 us (3%)
    all_to_all x1, waiting for transfers between devices, local(): lax.all_to_all(spread(rotated_k), 'seq', split_axis=0, concat_axis=1, til...  100 us
    all_to_all x1, waiting for transfers between devices, local(): lax.all_to_all(spread(value_states), 'seq', split_axis=0, concat_axis=1,...  96.1 us
    all_to_all x1, blocking collectives, local(): lax.all_to_all(attended, 'seq', split_axis=0, concat_axis=0, tiled=True)  26.4 us
    reduce_scatter x1, waiting for transfers between devices, local(): lax.psum_scatter(partial_value, 'tp', scatter_dimension=1, tiled=True)  20.8 us
    all_to_all x1, starting transfers between devices, local(): lax.all_to_all(query_send, 'seq', split_axis=0, concat_axis=1, tiled=True)  20.6 us
    all_to_all x1, waiting for transfers between devices, local(): lax.all_to_all(query_send, 'seq', split_axis=0, concat_axis=1, tiled=True)  15.9 us
    all_to_all x1, starting transfers between devices, local(): lax.all_to_all(spread(value_states), 'seq', split_axis=0, concat_axis=1,...  10.2 us
    dot_general x1, matrix products, attend_block(): jnp.dot(query_block, key_item.T, preferred_element_type=jnp.float32)  8.83 us
  transfers between devices with their start and end apart: 5, of which 4 were waited for; matrix products, arithmetic and copies ran while one was open for 8% of the time, Pallas kernels for 0%

commit v1 on v0

v1 whole, which is shorter than its diff:
```python
import functools
import math

import jax
import jax.numpy as jnp
import numpy as np
from jax import lax
from jax.experimental import pallas as pl
from jax.experimental.pallas import tpu as pltpu
from jax.sharding import PartitionSpec as P

DH = 128
PLANES = 16
LANES = 8
HALVES = 2
PIECE = 32
QUERY_ROWS = 128

masked_score = -1e30


def rotary(states, positions):
    quarter = DH // 4
    frequency = 100.0 ** (-jnp.arange(quarter, dtype=jnp.float32) / quarter)
    angles = positions.astype(jnp.float32)[:, :, None] * frequency
    angles = jnp.moveaxis(angles, 0, 1)
    cosine = jnp.cos(angles)[:, None, :, None, :]
    sine_table = jnp.sin(angles)[:, None, :, None, :]
    local_span, feature_width = states.shape
    shaped = states.reshape(local_span, feature_width // DH, 2, 2, quarter)
    partner = jnp.flip(shaped, axis=3)
    signed = jnp.array([-1.0, 1.0], jnp.float32)[:, None]
    rotated = shaped * cosine + partner * sine_table * signed
    return rotated.reshape(local_span, feature_width)


def attend_kernel(low_ref, high_ref, q_ref, kv_ref, qseg_ref, kseg_ref, out_ref, score_ref):
    scale = DH ** (-0.5) * math.log2(math.e)
    members = kv_ref.shape[0]
    keys = members * PIECE
    for tile in range(q_ref.shape[0] // QUERY_ROWS):
        rows = pl.ds(tile * QUERY_ROWS, QUERY_ROWS)
        query = q_ref[rows, :]
        query_segment = qseg_ref[rows, :]
        low, high = low_ref[tile], high_ref[tile]

        def score_step(plane, peak):
            start = pl.multiple_of(plane * PIECE, PIECE)
            key = kv_ref[:, 0, pl.ds(start, PIECE), :].reshape(keys, DH)
            score = lax.dot_general(
                query, key, (((1,), (1,)), ((), ())), preferred_element_type=jnp.float32
            )
            score = jnp.where(query_segment == kseg_ref[plane], score, masked_score)
            score_ref[plane] = score
            for part in range(keys // DH):
                peak = jnp.maximum(peak, score[:, part * DH:(part + 1) * DH])
            return peak

        peak = lax.fori_loop(
            low, high, score_step, jnp.full((QUERY_ROWS, DH), masked_score, jnp.float32)
        )
        peak = jnp.max(peak, axis=1, keepdims=True)

        def value_step(plane, carry):
            total, weighted = carry
            start = pl.multiple_of(plane * PIECE, PIECE)
            value = kv_ref[:, 1, pl.ds(start, PIECE), :].reshape(keys, DH)
            exponent = jnp.exp2((score_ref[plane] - peak) * scale)
            for part in range(keys // DH):
                total = total + exponent[:, part * DH:(part + 1) * DH]
            weighted = weighted + jnp.dot(
                exponent.astype(jnp.bfloat16), value, preferred_element_type=jnp.float32
            )
            return total, weighted

        zero = jnp.zeros((QUERY_ROWS, DH), jnp.float32)
        total, weighted = lax.fori_loop(low, high, value_step, (zero, zero))
        total = jnp.sum(total, axis=1, keepdims=True)
        out_ref[rows, :] = (weighted / total).astype(out_ref.dtype)


def attend(query, key_value, query_segment, key_segment, low, high):
    smem = pl.BlockSpec(memory_space=pltpu.SMEM)
    vmem = pl.BlockSpec(memory_space=pltpu.VMEM)
    keys = key_value.shape[0] * PIECE
    return pl.pallas_call(
        attend_kernel,
        out_shape=jax.ShapeDtypeStruct(query.shape, jnp.bfloat16),
        in_specs=[smem, smem, vmem, vmem, vmem, vmem],
        out_specs=vmem,
        scratch_shapes=[pltpu.VMEM((PLANES, QUERY_ROWS, keys), jnp.float32)],
        compiler_params=pltpu.CompilerParams(vmem_limit_bytes=40 * 1024 * 1024),
        cost_estimate=pl.CostEstimate(
            flops=4 * query.shape[0] * keys * PLANES * DH // 2,
            bytes_accessed=key_value.size * 2,
            transcendentals=query.shape[0] * keys * PLANES // 2,
        ),
    )(low, high, query, key_value, query_segment, key_segment)


def local(
    query_states,
    key_states,
    value_states,
    residual,
    segment_ids,
    positions,
    out_weight,
    layer_scale,
):
    local_span, feature_width = query_states.shape
    heads = feature_width // DH
    seq_count = lax.axis_size("seq")
    tp_count = lax.axis_size("tp")
    members = seq_count // heads
    seq_here = lax.axis_index("seq")

    by_column = seq_count // tp_count
    moves = []
    for block in range(tp_count):
        for source in range(tp_count):
            for i in range(by_column):
                moves.append(
                    ((block * by_column + i) * tp_count + source, (source * by_column + i) * tp_count + block)
                )
    weight = lax.ppermute(out_weight.T, ("seq", "tp"), moves)
    weight = lax.all_gather(weight, "seq", axis=0, tiled=True)
    weight = weight.reshape(tp_count, feature_width, feature_width)

    rotated_q = rotary(query_states.astype(jnp.float32), positions).astype(jnp.bfloat16)
    rotated_k = rotary(key_states.astype(jnp.float32), positions).astype(jnp.bfloat16)

    def chunk(states):
        return states.reshape(HALVES, PIECE, heads, DH).transpose(2, 0, 1, 3)

    sent = jnp.stack([chunk(rotated_q), chunk(rotated_k), chunk(value_states)], axis=2)
    sent = sent.reshape(PLANES, 3, PIECE, DH)
    rings = [[z * LANES + lane for z in range(PLANES)] for lane in range(LANES)]
    got = lax.all_to_all(sent, "seq", 0, 0, tiled=True, axis_index_groups=rings)
    query = got[:, 0].reshape(PLANES * PIECE, DH)
    key_value = got[:, 1:].transpose(1, 0, 2, 3).reshape(2, PLANES * PIECE, DH)
    squads = [[h * members + m for m in range(members)] for h in range(heads)]
    key_value = lax.all_gather(key_value, "seq", axis_index_groups=squads)

    grid = segment_ids.reshape(PLANES, LANES, HALVES, PIECE)
    key_segment = grid.transpose(0, 2, 1, 3).reshape(PLANES, 1, members * PIECE)
    half_here = (seq_here // LANES) % HALVES
    lane_here = seq_here % LANES
    query_segment = lax.dynamic_slice(
        grid, (0, lane_here, half_here, 0), (PLANES, 1, 1, PIECE)
    ).reshape(PLANES * PIECE)
    ends = query_segment.reshape(-1, QUERY_ROWS)
    plane_span = LANES * HALVES * PIECE
    low = jnp.sum(segment_ids[None, :] < ends[:, :1], axis=1, dtype=jnp.int32) // plane_span
    high = (
        jnp.sum(segment_ids[None, :] <= ends[:, -1:], axis=1, dtype=jnp.int32) + plane_span - 1
    ) // plane_span

    attended = attend(query, key_value, query_segment[:, None], key_segment, low, high)
    returned = lax.all_to_all(
        attended.reshape(PLANES, PIECE, DH), "seq", 0, 0, tiled=True, axis_index_groups=rings
    )
    returned = returned.reshape(heads, HALVES, PIECE, DH).transpose(1, 2, 0, 3)
    returned = returned.reshape(local_span, feature_width)
    gathered = lax.all_gather(returned, "tp")
    projected = lax.dot_general(
        gathered, weight, (((0, 2), (0, 2)), ((), ())), preferred_element_type=jnp.float32
    )
    encoded = residual.astype(jnp.float32) + layer_scale * projected
    return encoded.astype(jnp.bfloat16)


def solution(mesh):
    in_specs = (
        P("seq", "tp"),
        P("seq", "tp"),
        P("seq", "tp"),
        P("seq", "tp"),
        P(),
        P(None, "seq"),
        P("tp", "seq"),
        P("tp"),
    )
    out_specs = P("seq", "tp")
    return jax.shard_map(local, mesh=mesh, in_specs=in_specs, out_specs=out_specs, check_vma=False)
```

time: 360 us -> 259 us (0.72)
  waiting for transfers between devices: 234 us -> 141 us
  blocking collectives: 26.4 us -> 69.4 us
  starting transfers between devices: 38.2 us -> 0.71 us
  matrix products: 24 us -> 6.7 us
  Pallas kernels: 0 us -> 15.6 us
  other arithmetic: 11.7 us -> 2.31 us
    all_to_all x3 -> x0, waiting for transfers between devices: 212 us -> none  [the longest x1 100 us: local(): lax.all_to_all(spread(rotated_k), 'seq', split_axis=0, concat_axis=1, til...]
    all_gather x1 -> x2, waiting for transfers between devices: 0.02 us -> 141 us  [the longest x1 97 us: local(): weight = lax.all_gather(weight, 'seq', axis=0, tiled=True)]
    all_to_all x3 -> x0, starting transfers between devices: 37.9 us -> none  [the longest x1 20.6 us: local(): lax.all_to_all(query_send, 'seq', split_axis=0, concat_axis=1, tiled=True)]
    all_to_all x1 -> x2, blocking collectives: 26.4 us -> 57.4 us  [the longest x1 33.5 us: local(): got = lax.all_to_all(sent, 'seq', 0, 0, tiled=True, axis_index_groups=rings)]
    reduce_scatter x1 -> x0, waiting for transfers between devices: 20.8 us -> none  [local(): lax.psum_scatter(partial_value, 'tp', scatter_dimension=1, tiled=True)]
    dot_general x3 -> x1, matrix products: 24 us -> 6.7 us  [local(): lax.dot_general(gathered, weight, (((0, 2), (0, 2)), ((), ())), preferred...]
    pallas_call x0 -> x1, Pallas kernels: none -> 15.6 us  [attend(): pl.pallas_call(attend_kernel, out_shape=jax.ShapeDtypeStruct(query.shape,...]
    all_gather x0 -> x1, blocking collectives: none -> 12.1 us  [local(): gathered = lax.all_gather(returned, 'tp')]
  transfers between devices with their start and end apart: 5 -> 3, of which waited for: 4 -> 2; matrix products, arithmetic and copies ran while one was open for 8% -> 1% of each run, Pallas kernels for 0% -> 6%
where the time goes in v1:
time: 259 us
  waiting for transfers between devices  141 us (54%)
  blocking collectives  69.4 us (27%)
  Pallas kernels  15.6 us (6%)
  between operations  13.7 us (5%)
  local copies, waits for them, and re-layouts  9.92 us (4%)
  matrix products  6.7 us (3%)
    all_gather x1, waiting for transfers between devices, local(): weight = lax.all_gather(weight, 'seq', axis=0, tiled=True)  97 us
    all_gather x1, waiting for transfers between devices, local(): key_value = lax.all_gather(key_value, 'seq', axis_index_groups=squads)  43.6 us
    all_to_all x1, blocking collectives, local(): got = lax.all_to_all(sent, 'seq', 0, 0, tiled=True, axis_index_groups=rings)  33.5 us
    all_to_all x1, blocking collectives, local(): lax.all_to_all(attended.reshape(PLANES, PIECE, DH), 'seq', 0, 0, tiled=Tr...  23.8 us
    pallas_call x1, Pallas kernels, attend(): pl.pallas_call(attend_kernel, out_shape=jax.ShapeDtypeStruct(query.shape,...  15.6 us
    all_gather x1, blocking collectives, local(): gathered = lax.all_gather(returned, 'tp')  12.1 us
    dot_general x1, matrix products, local(): lax.dot_general(gathered, weight, (((0, 2), (0, 2)), ((), ())), preferred...  6.7 us
    unnamed x16, local copies, waits for them, and re-layouts  6.63 us
  transfers between devices with their start and end apart: 3, of which 2 were waited for; matrix products, arithmetic and copies ran while one was open for 1% of the time, Pallas kernels for 6%

profile of v1, /device:TPU:1, one launch (start us, length us, event | category | flops | bytes accessed | tf_op | source)
XLA Modules:
  0.0 259.0 jit_solution(15910670776581342313)
XLA Ops:
  6.6 0.7 convert_bitcast_fusion
  7.3 1.1 copy.57
  8.4 1.1 copy.60
  9.8 0.9 add_convert_fusion.1
  10.7 0.2 reshape.78
  11.0 0.3 copy.72
  11.3 0.2 reshape.77
  11.6 0.3 copy.70
  11.9 0.9 copy.74
  12.9 33.5 %all_to_all.10 = bf16[16,3,32,128]{3,2,1,0:T(8,128)(2,1)S(1)} all-to-all(bf16[16,3,32,128]{3,2,1,0:T(8,128)(2,1)S(1)} %copy.64), channel_id=1, replica_groups={{0,32,64,96,128,160,192,224,256,288,320,352,384,416,448,480},{4,36,68,1..., dimensions={0} | all-to-all | bytes 786432 | tf_op jit(solution)/shard_map/all_to_all | solution.py:139
  46.5 0.7 copy.73
  47.3 0.7 collective-permute-start
  48.0 0.6 copy-done.3
  48.9 0.5 broadcast.79
  49.4 0.6 fusion.3
  50.0 0.3 broadcast_in_dim_reshape.4.qseg_ref
  50.7 0.3 convert_reduce_fusion
  51.0 43.6 %all-gather.3.cloned.1.call-done.kv_ref = bf16[16,2,512,128]{3,2,1,0:T(8,128)(2,1)} async-done(((bf16[1,2,512,128]{3,2,1,0:T(8,128)(2,1)}), bf16[16,2,512,128]{3,2,1,0:T(8,128)(2,1)}) %all-gather.3.cloned.1.call-update) | async-done | bytes 4194320 | tf_op jit(solution)/shard_map/all_gather | solution.py:143
  94.6 2.2 copy-done
  96.8 15.6 %shard_map.100 = bf16[512,128]{1,0:T(8,128)(2,1)S(1)} custom-call(s32[4]{0:T(128)S(1)} %get-tuple-element.16.low_ref, s32[4]{0:T(128)S(1)} %get-tuple-element.15.high_ref, bf16[512,128]{1,0:T(8,128)(2,1)S(1)} %bitcast.55, bf16[16,2,512,128]{3,2,1,0:T(8,128)(2,1)S(1)} %copy-done, s32[512,1]{1,0:T(8,128)S(1)} %broadcast_in_dim_reshape.4.qseg_ref, ...), custom_call_target="tpu_custom_call" | custom-call | flops 1073741824 | bytes 4194304 | tf_op jit(solution)/shard_map/pallas_call | solution.py:86
  112.4 23.8 %all_to_all.11 = bf16[16,32,128]{2,1,0:T(8,128)(2,1)S(1)} all-to-all(bf16[16,32,128]{2,1,0:T(8,128)(2,1)S(1)} %bitcast.56), channel_id=1, replica_groups={{0,32,64,96,128,160,192,224,256,288,320,352,384,416,448,480},{4,36,68,1..., dimensions={0} | all-to-all | bytes 262144 | tf_op jit(solution)/shard_map/all_to_all | solution.py:160
  136.3 12.1 %all_gather.10 = bf16[4,64,1024]{2,1,0:T(8,128)(2,1)S(1)} all-gather(bf16[1,64,1024]{2,1,0:T(8,128)(2,1)S(1)} %all_gather_reshape.7), channel_id=1, replica_groups=mesh['seq'=128,'tp'=4] {'tp'}, dimensions={0}, use_global_device_ids=true | all-gather | bytes 655360 | tf_op jit(solution)/shard_map/all_gather | solution.py:165
  148.4 97.0 %all-gather.5.cloned.1.call-done = bf16[4096,1024]{1,0:T(8,128)(2,1)} async-done(((bf16[32,1024]{1,0:T(8,128)(2,1)}), bf16[4096,1024]{1,0:T(8,128)(2,1)}) %all-gather.5.cloned.1.call-update) | async-done | bytes 8388624 | tf_op jit(solution)/shard_map/all_gather | solution.py:127
  245.5 6.7 %fusion.2 = bf16[64,1024]{1,0:T(8,128)(2,1)} fusion(bf16[4,64,1024]{2,1,0:T(8,128)(2,1)S(1)} %all_gather.10, bf16[4,1024,1024]{2,1,0:T(8,128)(2,1)} %bitcast.57, bf16[64,1024]{1,0:T(8,128)(2,1)S(1)} %copy-done.1, f32[1024]{0:T(1024)S(1)} %copy-done.4), kind=kOutput, calls=%fused_computation.3 | convolution fusion | flops 537133056 | bytes 9179136 | tf_op jit(solution)/shard_map/dot_general | solution.py:166
  (32 shorter events, 1.2 us)
Async XLA Ops:
  6.5 40.8 %copy-start.5 = (bf16[1024,32]{0,1:T(8,128)(2,1)S(1)}, bf16[1024,32]{0,1:T(8,128)(2,1)}, u32[]{:S(2)}) copy-start(bf16[1024,32]{0,1:T(8,128)(2,1)} %param.16) | copy-start | bytes 196612
  6.5 42.2 %copy-start.2 = (s32[8192]{0:T(1024)S(1)}, s32[8192]{0:T(1024)}, u32[]{:S(2)}) copy-start(s32[8192]{0:T(1024)} %param.14) | copy-start | bytes 98308
  6.5 88.1 %all-gather.3.cloned.1.call-start = ((), (), s32[]{:S(2)}) async-start(), calls=%async_computation.2 | async-start | bytes 4456448 | tf_op jit(solution)/shard_map/all_gather | solution.py:143
  9.5 236.0 %copy-start.1 = (bf16[64,1024]{1,0:T(8,128)(2,1)S(1)}, bf16[64,1024]{1,0:T(8,128)(2,1)}, u32[]{:S(2)}) copy-start(bf16[64,1024]{1,0:T(8,128)(2,1)} %param.13) | copy-start | bytes 393220
  9.5 236.0 %copy-start.4 = (f32[1024]{0:T(1024)S(1)}, f32[1024]{0:T(1024)}, u32[]{:S(2)}) copy-start(f32[1024]{0:T(1024)} %param.17) | copy-start | bytes 12292
  47.3 198.2 %all-gather.5.cloned.1.call-start = ((), (), s32[]{:S(2)}) async-start(), calls=%async_computation.3 | async-start | bytes 8454144 | tf_op jit(solution)/shard_map/all_gather | solution.py:127
  47.3 0.7 collective-permute-start
  48.0 0.6 copy-start.3
  94.6 2.2 copy-start
Sparse Core Ops, SparseCore 0:
  47.4 47.1 all-gather.2
  97.7 147.6 all-gather.4

commit v2 on v1

--- a/solution.py
+++ b/solution.py
@@ -1,9 +1,7 @@
-import functools
 import math
 
 import jax
 import jax.numpy as jnp
-import numpy as np
 from jax import lax
 from jax.experimental import pallas as pl
 from jax.experimental.pallas import tpu as pltpu
@@ -15,6 +13,8 @@
 HALVES = 2
 PIECE = 32
 QUERY_ROWS = 128
+
+MESH = pl.DeviceIdType.MESH
 
 masked_score = -1e30
 
@@ -98,6 +98,179 @@
     )(low, high, query, key_value, query_segment, key_segment)
 
 
+def finish_kernel(
+    attended_ref,
+    weight_ref,
+    residual_ref,
+    gain_ref,
+    encoded_ref,
+    plane_buf,
+    part_buf,
+    share_buf,
+    z_send,
+    z_recv,
+    lane_send,
+    lane_recv,
+    share_send,
+    share_recv,
+):
+    seq_here, tp_here = lax.axis_index("seq"), lax.axis_index("tp")
+    z, lane = seq_here // LANES, seq_here % LANES
+    block = lane // 2
+    feeds_itself = jnp.where(block == tp_here, 1, 0)
+
+    def along_z(step):
+        return (z + step) % PLANES
+
+    def in_plane(step):
+        return (lane + step) % LANES
+
+    def z_copy(source, dest):
+        return pltpu.make_async_remote_copy(
+            src_ref=attended_ref.at[dest],
+            dst_ref=plane_buf.at[lane, source],
+            send_sem=z_send.at[dest],
+            recv_sem=z_recv.at[source],
+            device_id=(dest * LANES + lane, tp_here),
+            device_id_type=MESH,
+        )
+
+    def lane_copy(source, dest):
+        return pltpu.make_async_remote_copy(
+            src_ref=plane_buf.at[source],
+            dst_ref=plane_buf.at[source],
+            send_sem=lane_send.at[dest],
+            recv_sem=lane_recv.at[source],
+            device_id=(z * LANES + dest, tp_here),
+            device_id_type=MESH,
+        )
+
+    def share_copy(source, dest):
+        return pltpu.make_async_remote_copy(
+            src_ref=part_buf.at[dest],
+            dst_ref=share_buf.at[source],
+            send_sem=share_send.at[dest],
+            recv_sem=share_recv.at[source],
+            device_id=(z * LANES + dest, block),
+            device_id_type=MESH,
+        )
+
+    def each(start, stop, act):
+        def body(step, carry):
+            act(step)
+            return carry
+
+        lax.fori_loop(start, stop, body, 0)
+
+    barrier = pltpu.get_barrier_semaphore()
+
+    def greet(seq, tp):
+        pl.semaphore_signal(barrier, inc=1, device_id=(seq, tp), device_id_type=MESH)
+
+    each(1, PLANES, lambda step: greet(along_z(step) * LANES + lane, tp_here))
+    each(1, LANES, lambda step: greet(z * LANES + in_plane(step), tp_here))
+
+    def greet_feeder(source):
+        feeder_tp, feeder_lane = source // 2, 2 * tp_here + source % 2
+
+        @pl.when(jnp.logical_or(feeder_tp != tp_here, feeder_lane != lane))
+        def _():
+            greet(z * LANES + feeder_lane, feeder_tp)
+
+    each(0, LANES, greet_feeder)
+    pl.semaphore_wait(barrier, PLANES - 1 + LANES - 1 + LANES - feeds_itself)
+
+    each(1, PLANES, lambda step: z_copy(z, along_z(step)).start())
+    plane_buf[lane, z] = attended_ref[z]
+    each(1, PLANES, lambda step: z_copy(along_z(step), z).wait_recv())
+
+    each(1, LANES, lambda step: lane_copy(lane, in_plane(step)).start())
+    each(1, LANES, lambda step: lane_copy(in_plane(step), lane).wait_recv())
+
+    per_step = 4
+    heads = PLANES // HALVES
+    rows = per_step * HALVES * PIECE
+    for step in range(LANES // per_step):
+        token = plane_buf[step * per_step:(step + 1) * per_step]
+        token = jnp.concatenate(
+            [token[:, HALVES * h:HALVES * (h + 1)].reshape(rows, DH) for h in range(heads)], axis=1
+        )
+        part = lax.dot_general(
+            token, weight_ref[...], (((1,), (1,)), ((), ())), preferred_element_type=jnp.float32
+        )
+        part_buf[step * per_step:(step + 1) * per_step] = part.astype(jnp.bfloat16).reshape(
+            per_step, HALVES * PIECE, part.shape[1]
+        )
+
+    own_source = tp_here * 2 + lane % 2
+
+    def share_out(step):
+        dest = in_plane(step)
+
+        @pl.when(jnp.logical_or(block != tp_here, dest != lane))
+        def _():
+            share_copy(own_source, dest).start()
+
+        @pl.when(jnp.logical_and(block == tp_here, dest == lane))
+        def _():
+            share_buf[own_source] = part_buf[dest]
+
+    each(0, LANES, share_out)
+
+    def collect(source):
+        feeder_tp, feeder_lane = source // 2, 2 * tp_here + source % 2
+
+        @pl.when(jnp.logical_or(feeder_tp != tp_here, feeder_lane != lane))
+        def _():
+            share_copy(source, lane).wait_recv()
+
+    each(0, LANES, collect)
+    width = part_buf.shape[2]
+    for half in range(2):
+        columns = slice(half * width, (half + 1) * width)
+        total = share_buf[half].astype(jnp.float32)
+        for source in range(1, LANES // 2):
+            total = total + share_buf[2 * source + half].astype(jnp.float32)
+        encoded = residual_ref[:, columns].astype(jnp.float32) + gain_ref[:, columns] * total
+        encoded_ref[:, columns] = encoded.astype(encoded_ref.dtype)
+
+    each(1, PLANES, lambda step: z_copy(z, along_z(step)).wait_send())
+    each(1, LANES, lambda step: lane_copy(lane, in_plane(step)).wait_send())
+
+    def share_sent(step):
+        dest = in_plane(step)
+
+        @pl.when(jnp.logical_or(block != tp_here, dest != lane))
+        def _():
+            share_copy(own_source, dest).wait_send()
+
+    each(0, LANES, share_sent)
+
+
+def finish(attended, weight, residual, gain):
+    vmem = pl.BlockSpec(memory_space=pltpu.VMEM)
+    return pl.pallas_call(
+        finish_kernel,
+        out_shape=jax.ShapeDtypeStruct(residual.shape, jnp.bfloat16),
+        in_specs=[vmem] * 4,
+        out_specs=vmem,
+        scratch_shapes=[
+            pltpu.VMEM((LANES, PLANES, PIECE, DH), jnp.bfloat16),
+            pltpu.VMEM((LANES, HALVES * PIECE, weight.shape[0]), jnp.bfloat16),
+            pltpu.VMEM((LANES, HALVES * PIECE, weight.shape[0]), jnp.bfloat16),
+            pltpu.SemaphoreType.DMA((PLANES,)),
+            pltpu.SemaphoreType.DMA((PLANES,)),
+            pltpu.SemaphoreType.DMA((LANES,)),
+            pltpu.SemaphoreType.DMA((LANES,)),
+            pltpu.SemaphoreType.DMA((LANES,)),
+            pltpu.SemaphoreType.DMA((LANES,)),
+        ],
+        compiler_params=pltpu.CompilerParams(
+            collective_id=1, has_side_effects=True, vmem_limit_bytes=32 * 1024 * 1024
+        ),
+    )(attended, weight, residual, gain)
+
+
 def local(
     query_states,
     key_states,
@@ -111,21 +284,15 @@
     local_span, feature_width = query_states.shape
     heads = feature_width // DH
     seq_count = lax.axis_size("seq")
-    tp_count = lax.axis_size("tp")
     members = seq_count // heads
     seq_here = lax.axis_index("seq")
 
-    by_column = seq_count // tp_count
-    moves = []
-    for block in range(tp_count):
-        for source in range(tp_count):
-            for i in range(by_column):
-                moves.append(
-                    ((block * by_column + i) * tp_count + source, (source * by_column + i) * tp_count + block)
-                )
-    weight = lax.ppermute(out_weight.T, ("seq", "tp"), moves)
-    weight = lax.all_gather(weight, "seq", axis=0, tiled=True)
-    weight = weight.reshape(tp_count, feature_width, feature_width)
+    rings = [[z * LANES + lane for z in range(PLANES)] for lane in range(LANES)]
+    moves = [
+        (lane * PLANES + z, z * LANES + lane) for lane in range(LANES) for z in range(PLANES)
+    ]
+    weight = lax.ppermute(out_weight.T, "seq", moves)
+    weight = lax.all_gather(weight, "seq", axis_index_groups=rings, axis=0, tiled=True)
 
     rotated_q = rotary(query_states.astype(jnp.float32), positions).astype(jnp.bfloat16)
     rotated_k = rotary(key_states.astype(jnp.float32), positions).astype(jnp.bfloat16)
@@ -135,7 +302,6 @@
 
     sent = jnp.stack([chunk(rotated_q), chunk(rotated_k), chunk(value_states)], axis=2)
     sent = sent.reshape(PLANES, 3, PIECE, DH)
-    rings = [[z * LANES + lane for z in range(PLANES)] for lane in range(LANES)]
     got = lax.all_to_all(sent, "seq", 0, 0, tiled=True, axis_index_groups=rings)
     query = got[:, 0].reshape(PLANES * PIECE, DH)
     key_value = got[:, 1:].transpose(1, 0, 2, 3).reshape(2, PLANES * PIECE, DH)
@@ -157,17 +323,9 @@
     ) // plane_span
 
     attended = attend(query, key_value, query_segment[:, None], key_segment, low, high)
-    returned = lax.all_to_all(
-        attended.reshape(PLANES, PIECE, DH), "seq", 0, 0, tiled=True, axis_index_groups=rings
+    return finish(
+        attended.reshape(PLANES, PIECE, DH), weight, residual, layer_scale[None, :]
     )
-    returned = returned.reshape(heads, HALVES, PIECE, DH).transpose(1, 2, 0, 3)
-    returned = returned.reshape(local_span, feature_width)
-    gathered = lax.all_gather(returned, "tp")
-    projected = lax.dot_general(
-        gathered, weight, (((0, 2), (0, 2)), ((), ())), preferred_element_type=jnp.float32
-    )
-    encoded = residual.astype(jnp.float32) + layer_scale * projected
-    return encoded.astype(jnp.bfloat16)
 
 
 def solution(mesh):

time: 259 us -> 229 us (0.88)
  Pallas kernels: 15.6 us -> 77.7 us
  waiting for transfers between devices: 141 us -> 80.3 us
  blocking collectives: 69.4 us -> 33.7 us
  starting transfers between devices: 0.71 us -> 8.33 us
  matrix products: 6.7 us -> 0 us
    pallas_call x0 -> x1, Pallas kernels: none -> 61.4 us  [finish(): pl.pallas_call(finish_kernel, out_shape=jax.ShapeDtypeStruct(residual.sha...]
    all_gather x1, waiting for transfers between devices: 97 us -> 44.5 us  [local(): lax.all_gather(weight, 'seq', axis_index_groups=rings, axis=0, tiled=True)]
    all_to_all x1 -> x0, blocking collectives: 23.8 us -> none  [local(): lax.all_to_all(attended.reshape(PLANES, PIECE, DH), 'seq', 0, 0, tiled=Tr...]
    all_gather x1 -> x0, blocking collectives: 12.1 us -> none  [local(): gathered = lax.all_gather(returned, 'tp')]
    all_gather x1, waiting for transfers between devices: 43.6 us -> 32 us  [local(): key_value = lax.all_gather(key_value, 'seq', axis_index_groups=squads)]
    ppermute x1, starting transfers between devices: 0.66 us -> 8.29 us  [local(): weight = lax.ppermute(out_weight.T, 'seq', moves)]
    dot_general x1 -> x0, matrix products: 6.7 us -> none  [local(): lax.dot_general(gathered, weight, (((0, 2), (0, 2)), ((), ())), preferred...]
    ppermute x1, waiting for transfers between devices: 0.01 us -> 3.81 us  [local(): weight = lax.ppermute(out_weight.T, 'seq', moves)]
  transfers between devices with their start and end apart: 3 -> 3, of which waited for: 2 -> 3; matrix products, arithmetic and copies ran while one was open for 1% -> 1% of each run, Pallas kernels for 6% -> 7%
where the time goes in v2:
time: 229 us; the launch traced here: 228 us
  waiting for transfers between devices  80.3 us (35%)
  Pallas kernels  77.7 us (34%)
  blocking collectives  33.7 us (15%)
  between operations  13.7 us (6%)
  local copies, waits for them, and re-layouts  11.7 us (5%)
  starting transfers between devices  8.33 us (4%)
  other arithmetic  2.29 us (1%)
    pallas_call x1, Pallas kernels, finish(): pl.pallas_call(finish_kernel, out_shape=jax.ShapeDtypeStruct(residual.sha...  61.4 us
    all_gather x1, waiting for transfers between devices, local(): lax.all_gather(weight, 'seq', axis_index_groups=rings, axis=0, tiled=True)  44.5 us
    all_to_all x1, blocking collectives, local(): got = lax.all_to_all(sent, 'seq', 0, 0, tiled=True, axis_index_groups=rings)  33.7 us
    all_gather x1, waiting for transfers between devices, local(): key_value = lax.all_gather(key_value, 'seq', axis_index_groups=squads)  32 us
    pallas_call x1, Pallas kernels, attend(): pl.pallas_call(attend_kernel, out_shape=jax.ShapeDtypeStruct(query.shape,...  16.4 us
    unnamed x19, local copies, waits for them, and re-layouts  8.51 us
    ppermute x1, starting transfers between devices, local(): weight = lax.ppermute(out_weight.T, 'seq', moves)  8.29 us
  transfers between devices with their start and end apart: 3, of which 3 were waited for; matrix products, arithmetic and copies ran while one was open for 1% of the time, Pallas kernels for 7%

profile of v2, /device:TPU:1, one launch (start us, length us, event | category | flops | bytes accessed | tf_op | source)
XLA Modules:
  0.0 227.7 jit_solution(5453136010202032304)
XLA Ops:
  6.5 0.9 copy.68
  7.5 1.1 copy.52
  8.6 0.7 convert_bitcast_fusion
  9.3 1.1 copy.55
  10.7 0.9 add_convert_fusion.1
  11.6 0.2 reshape.68
  11.9 0.3 copy.66
  12.5 0.3 copy.64
  12.9 33.7 %all_to_all.5 = bf16[16,3,32,128]{3,2,1,0:T(8,128)(2,1)S(1)} all-to-all(bf16[16,3,32,128]{3,2,1,0:T(8,128)(2,1)S(1)} %copy.59), channel_id=1, replica_groups={{0,32,64,96,128,160,192,224,256,288,320,352,384,416,448,480},{4,36,68,1..., dimensions={0} | all-to-all | bytes 786432 | tf_op jit(solution)/shard_map/all_to_all | solution.py:305
  46.6 0.7 copy.67
  47.4 8.3 %collective-permute-start = (bf16[32,1024]{1,0:T(8,128)(2,1)S(1)}, bf16[32,1024]{1,0:T(8,128)(2,1)S(1)}, u32[]{:S(2)}, u32[]{:S(2)}) collective-permute-start(bf16[32,1024]{1,0:T(8,128)(2,1)S(1)} %bitcast.52), channel_id=1, source_target_pairs={{0,0},{4,32},{8,64},{12,96},{16,128},{20,160},{24,192},{28,224},{3... | collective-permute-start | bytes 196616 | tf_op jit(solution)/shard_map/ppermute | solution.py:294
  55.7 3.8 %collective-permute-done = bf16[32,1024]{1,0:T(8,128)(2,1)S(1)} collective-permute-done((bf16[32,1024]{1,0:T(8,128)(2,1)S(1)}, bf16[32,1024]{1,0:T(8,128)(2,1)S(1)}, u32[]{:S(2)}, u32[]{:S(2)}) %collective-permute-start) | collective-permute-done | bytes 65568 | tf_op jit(solution)/shard_map/ppermute | solution.py:294
  59.6 0.6 copy-done.5
  60.4 0.6 broadcast.78
  61.0 0.7 fusion
  61.7 0.3 broadcast_in_dim_reshape.4.qseg_ref
  62.3 0.3 convert_reduce_fusion
  62.6 32.0 %all-gather.3.cloned.1.call-done.kv_ref = bf16[16,2,512,128]{3,2,1,0:T(8,128)(2,1)} async-done(((bf16[1,2,512,128]{3,2,1,0:T(8,128)(2,1)}), bf16[16,2,512,128]{3,2,1,0:T(8,128)(2,1)}) %all-gather.3.cloned.1.call-update) | async-done | bytes 4194320 | tf_op jit(solution)/shard_map/all_gather | solution.py:309
  94.6 2.2 copy-done
  96.8 16.4 %shard_map.100 = bf16[512,128]{1,0:T(8,128)(2,1)S(1)} custom-call(s32[4]{0:T(128)S(1)} %get-tuple-element.16.low_ref, s32[4]{0:T(128)S(1)} %get-tuple-element.15.high_ref, bf16[512,128]{1,0:T(8,128)(2,1)S(1)} %bitcast.39, bf16[16,2,512,128]{3,2,1,0:T(8,128)(2,1)S(1)} %copy-done, s32[512,1]{1,0:T(8,128)S(1)} %broadcast_in_dim_reshape.4.qseg_ref, ...), custom_call_target="tpu_custom_call" | custom-call | flops 1073741824 | bytes 4194304 | tf_op jit(solution)/shard_map/pallas_call | solution.py:86
  113.2 44.5 %all-gather.5.cloned.1.call-done.weight_ref = bf16[512,1024]{1,0:T(8,128)(2,1)} async-done(((bf16[32,1024]{1,0:T(8,128)(2,1)}), bf16[512,1024]{1,0:T(8,128)(2,1)}) %all-gather.5.cloned.1.call-update) | async-done | bytes 1048592 | tf_op jit(solution)/shard_map/all_gather | solution.py:295
  157.7 1.2 copy-done.1
  158.9 61.4 %shard_map.101 = bf16[64,1024]{1,0:T(8,128)(2,1)S(1)} custom-call(bf16[16,32,128]{2,1,0:T(8,128)(2,1)S(1)} %bitcast.40, bf16[512,1024]{1,0:T(8,128)(2,1)S(1)} %copy-done.1, bf16[64,1024]{1,0:T(8,128)(2,1)S(1)} %copy-done.2, f32[1,1024]{1,0:T(1,128)S(1)} %bitcast.41), custom_call_target="tpu_custom_call" | custom-call | tf_op jit(solution)/shard_map/pallas_call | solution.py:252
  220.2 0.7 copy.70
  (31 shorter events, 1.3 us)
Async XLA Ops:
  6.5 88.1 %all-gather.3.cloned.1.call-start = ((), (), s32[]{:S(2)}) async-start(), calls=%async_computation.1 | async-start | bytes 4456448 | tf_op jit(solution)/shard_map/all_gather | solution.py:309
  10.5 37.0 %copy-start.6 = (bf16[1024,32]{0,1:T(8,128)(2,1)S(1)}, bf16[1024,32]{0,1:T(8,128)(2,1)}, u32[]{:S(2)}) copy-start(bf16[1024,32]{0,1:T(8,128)(2,1)} %param.16) | copy-start | bytes 196612
  10.7 49.6 %copy-start.4 = (s32[8192]{0:T(1024)S(1)}, s32[8192]{0:T(1024)}, u32[]{:S(2)}) copy-start(s32[8192]{0:T(1024)} %param.14) | copy-start | bytes 98308
  12.9 144.7 %copy-start.2 = (bf16[64,1024]{1,0:T(8,128)(2,1)S(1)}, bf16[64,1024]{1,0:T(8,128)(2,1)}, u32[]{:S(2)}) copy-start(bf16[64,1024]{1,0:T(8,128)(2,1)} %residual_ref.1) | copy-start | bytes 393220
  12.9 144.7 %copy-start.3 = (f32[1024]{0:T(1024)S(1)}, f32[1024]{0:T(1024)}, u32[]{:S(2)}) copy-start(f32[1024]{0:T(1024)} %param.17) | copy-start | bytes 12292
  47.4 110.3 %all-gather.5.cloned.1.call-start = ((), (), s32[]{:S(2)}) async-start(), calls=%async_computation.2 | async-start | bytes 1114112 | tf_op jit(solution)/shard_map/all_gather | solution.py:295
  47.4 12.1 %collective-permute-start = (bf16[32,1024]{1,0:T(8,128)(2,1)S(1)}, bf16[32,1024]{1,0:T(8,128)(2,1)S(1)}, u32[]{:S(2)}, u32[]{:S(2)}) collective-permute-start(bf16[32,1024]{1,0:T(8,128)(2,1)S(1)} %bitcast.52), channel_id=1, source_target_pairs={{0,0},{4,32},{8,64},{12,96},{16,128},{20,160},{24,192},{28,224},{3... | collective-permute-start | bytes 196616 | tf_op jit(solution)/shard_map/ppermute | solution.py:294
  59.5 0.6 copy-start.5
  94.6 2.2 copy-start
  157.7 1.2 copy-start.1
Sparse Core Ops, SparseCore 0:
  47.5 47.0 all-gather.2
  96.7 60.8 all-gather.4

commit v3 on v0

v3 whole, which is shorter than its diff:
```python
import math

import jax
import jax.numpy as jnp
from jax import lax
from jax.experimental import pallas as pl
from jax.experimental.pallas import tpu as pltpu
from jax.sharding import PartitionSpec as P

DH = 128
PLANES = 16
LANES = 8
GROUPS = 4
SPAN = 64
TOKENS = LANES * SPAN
CHUNK = 128
HALF_RING = PLANES // 2
EXPONENT_SCALE = DH ** (-0.5) * math.log2(math.e)
MESH = pl.DeviceIdType.MESH

masked_score = -1e30


def each(start, stop, act):
    def body(step, carry):
        act(step)
        return carry

    lax.fori_loop(start, stop, body, 0)


def layer_kernel(
    query_ref,
    key_ref,
    value_ref,
    residual_ref,
    segment_ref,
    position_ref,
    weight_ref,
    gain_ref,
    encoded_ref,
    send_buf,
    stage_buf,
    kv_buf,
    weight_buf,
    query_segment,
    peak_ref,
    total_ref,
    sum_ref,
    plane_buf,
    part_buf,
    share_buf,
    stage_send,
    stage_recv,
    ring_send,
    ring_recv,
    weight_send,
    weight_recv,
    plane_send,
    plane_recv,
    share_send,
    share_recv,
):
    seq_here, tp_here = lax.axis_index("seq"), lax.axis_index("tp")
    z, lane = seq_here // LANES, seq_here % LANES
    row, core = lane // 2, lane % 2
    inside = tp_here * LANES + lane
    crowd = GROUPS * LANES

    def plane_at(step):
        return (z + step + PLANES) % PLANES

    up = (plane_at(1) * LANES + lane, tp_here)
    down = (plane_at(-1) * LANES + lane, tp_here)

    barrier = pltpu.get_barrier_semaphore()

    def greet(device):
        pl.semaphore_signal(barrier, inc=1, device_id=device, device_id_type=MESH)

    greet(up)
    greet(down)

    def greet_inside(step):
        other = (inside + step) % crowd
        greet((z * LANES + other % LANES, other // LANES))

    each(1, crowd, greet_inside)

    def weight_copy(piece, way):
        return pltpu.make_async_remote_copy(
            src_ref=weight_buf.at[piece],
            dst_ref=weight_buf.at[piece],
            send_sem=weight_send.at[way, piece],
            recv_sem=weight_recv.at[piece],
            device_id=up if way == 0 else down,
            device_id_type=MESH,
        )

    def ring_copy(piece, which, way):
        return pltpu.make_async_remote_copy(
            src_ref=kv_buf.at[piece, which],
            dst_ref=kv_buf.at[piece, which],
            send_sem=ring_send.at[way, piece, which],
            recv_sem=ring_recv.at[piece, which],
            device_id=up if way == 0 else down,
            device_id_type=MESH,
        )

    def stage_copy(source, dest):
        return pltpu.make_async_remote_copy(
            src_ref=send_buf.at[dest],
            dst_ref=stage_buf.at[source],
            send_sem=stage_send.at[dest],
            recv_sem=stage_recv.at[source],
            device_id=(z * LANES + dest, tp_here),
            device_id_type=MESH,
        )

    def weight_step(step, last=False):
        weight_copy(plane_at(-step), 0).wait_recv()
        if not last:
            weight_copy(plane_at(-step), 0).start()
        weight_copy(plane_at(step), 1).wait_recv()

    weight_buf[z] = weight_ref[...]

    lanes = lax.broadcasted_iota(jnp.int32, (SPAN, DH), 1)
    frequency = jnp.exp((lanes % 32).astype(jnp.float32) * (-math.log(100.0) / 32))
    place = jnp.where(lanes < DH // 2, position_ref[:, 0:1], position_ref[:, 1:2])
    angle = place.astype(jnp.float32) * frequency
    first = lanes % 64 < 32
    cosine = jnp.cos(angle)
    sine = jnp.sin(angle)
    sine = jnp.where(first, -sine, sine)

    def rotate(states):
        states = states.astype(jnp.float32)
        partner = jnp.where(
            first, pltpu.roll(states, DH - 32, axis=1), pltpu.roll(states, 32, axis=1)
        )
        return (states * cosine + partner * sine).astype(jnp.bfloat16)

    pl.semaphore_wait(barrier, 2 + crowd - 1)
    weight_copy(z, 0).start()
    weight_copy(z, 1).start()

    for head in range(LANES):
        features = slice(head * DH, (head + 1) * DH)
        send_buf[head, 0] = rotate(query_ref[:, features])
        send_buf[head, 1] = rotate(key_ref[:, features])
        send_buf[head, 2] = value_ref[:, features]

        @pl.when(head != lane)
        def _(head=head):
            stage_copy(lane, head).start()

    stage_buf[lane] = send_buf[lane]

    for part in range(TOKENS // CHUNK):
        own = segment_ref[pl.ds(z * (TOKENS // CHUNK) + part, 1), :].astype(jnp.float32)
        query_segment[part * CHUNK:(part + 1) * CHUNK] = jnp.broadcast_to(own, (CHUNK, CHUNK)).T
    peak_ref[...] = jnp.full(peak_ref.shape, masked_score, jnp.float32)
    total_ref[...] = jnp.zeros(total_ref.shape, jnp.float32)
    sum_ref[...] = jnp.zeros(sum_ref.shape, jnp.float32)

    weight_copy(plane_at(-1), 0).wait_recv()
    weight_copy(plane_at(-1), 0).start()
    weight_copy(plane_at(1), 1).wait_recv()
    weight_copy(plane_at(1), 1).start()

    each(1, LANES, lambda step: stage_copy((lane + step) % LANES, lane).wait_recv())
    for which in range(2):
        kv_buf[z, which] = stage_buf[:, 1 + which].reshape(TOKENS, DH)
        for way in range(2):
            ring_copy(z, which, way).start()

    def attend(piece):
        key = kv_buf[piece, 0]
        value = kv_buf[piece, 1]
        parts = TOKENS // CHUNK
        key_segment = [
            segment_ref[pl.ds(piece * parts + part, 1), :].astype(jnp.float32)
            for part in range(parts)
        ]
        for chunk in range(parts):
            rows = slice(chunk * CHUNK, (chunk + 1) * CHUNK)
            per = CHUNK // SPAN
            query = stage_buf[chunk * per:(chunk + 1) * per, 0].reshape(CHUNK, DH)
            score = lax.dot_general(
                query, key, (((1,), (1,)), ((), ())), preferred_element_type=jnp.float32
            )
            segment = query_segment[rows]
            scores = [
                jnp.where(
                    segment == key_segment[part],
                    score[:, part * CHUNK:(part + 1) * CHUNK],
                    masked_score,
                )
                for part in range(parts)
            ]
            top = jnp.maximum(
                jnp.maximum(scores[0], scores[1]), jnp.maximum(scores[2], scores[3])
            )
            old = peak_ref[rows]
            peak = jnp.maximum(old, jnp.max(top, axis=1, keepdims=True))
            peak_ref[rows] = peak
            fade = jnp.exp2((old - peak) * EXPONENT_SCALE)
            exponents = [jnp.exp2((part - peak) * EXPONENT_SCALE) for part in scores]
            total_ref[rows] = total_ref[rows] * fade + (
                (exponents[0] + exponents[1]) + (exponents[2] + exponents[3])
            )
            weights = jnp.concatenate([part.astype(jnp.bfloat16) for part in exponents], axis=1)
            sum_ref[rows] = sum_ref[rows] * fade + jnp.dot(
                weights, value, preferred_element_type=jnp.float32
            )

    def ring_step(step):
        below, above = plane_at(-step), plane_at(step)
        open_still = step < HALF_RING - 1
        ring_copy(below, 0, 0).wait_recv()
        ring_copy(below, 0, 0).start()
        ring_copy(above, 0, 1).wait_recv()

        @pl.when(open_still)
        def _():
            ring_copy(above, 0, 1).start()

        attend(plane_at(step - 1))

        ring_copy(below, 1, 0).wait_recv()

        @pl.when(open_still)
        def _():
            ring_copy(below, 1, 0).start()

        ring_copy(above, 1, 1).wait_recv()
        ring_copy(above, 1, 1).start()

        @pl.when(open_still)
        def _():
            weight_copy(plane_at(-step - 1), 0).wait_recv()
            weight_copy(plane_at(-step - 1), 0).start()
            weight_copy(plane_at(step + 1), 1).wait_recv()

        @pl.when(step < HALF_RING - 2)
        def _():
            weight_copy(plane_at(step + 1), 1).start()

        attend(below)

    each(1, HALF_RING, ring_step)
    attend(plane_at(HALF_RING - 1))
    ring_copy(plane_at(HALF_RING), 0, 0).wait_recv()
    ring_copy(plane_at(HALF_RING), 1, 1).wait_recv()
    attend(plane_at(HALF_RING))

    total = jnp.sum(total_ref[...], axis=1, keepdims=True)
    plane_buf[lane] = (sum_ref[...] / total).astype(jnp.bfloat16)

    def plane_copy(slot, device_lane):
        return pltpu.make_async_remote_copy(
            src_ref=plane_buf.at[slot],
            dst_ref=plane_buf.at[slot],
            send_sem=plane_send.at[slot, device_lane],
            recv_sem=plane_recv.at[slot],
            device_id=(z * LANES + device_lane, tp_here),
            device_id_type=MESH,
        )

    sibling = row * 2 + 1 - core

    def mate(step):
        return ((row + step) % GROUPS) * 2 + core

    def sibling_of(step):
        return ((row + step) % GROUPS) * 2 + 1 - core

    each(1, GROUPS, lambda step: plane_copy(lane, mate(step)).start())
    plane_copy(lane, sibling).start()

    def pass_on(step):
        plane_copy(mate(step), lane).wait_recv()
        plane_copy(mate(step), sibling).start()

    each(1, GROUPS, pass_on)
    each(0, GROUPS, lambda step: plane_copy(sibling_of(step), lane).wait_recv())

    weight_copy(plane_at(HALF_RING), 0).wait_recv()
    weight = weight_buf[...].reshape(PLANES * weight_ref.shape[0], LANES * DH)
    rows = TOKENS // 2
    for half in range(2):
        token = jnp.concatenate(
            [plane_buf[head, half * rows:(half + 1) * rows] for head in range(LANES)], axis=1
        )
        part = lax.dot_general(
            token, weight, (((1,), (1,)), ((), ())), preferred_element_type=jnp.float32
        ).astype(jnp.bfloat16)
        for group in range(GROUPS):
            part_buf[group, half * (LANES // 2):(half + 1) * (LANES // 2)] = part[
                :, group * DH:(group + 1) * DH
            ].reshape(LANES // 2, SPAN, DH)

    def share_copy(source, dest):
        return pltpu.make_async_remote_copy(
            src_ref=part_buf.at[dest // LANES, dest % LANES],
            dst_ref=share_buf.at[source // LANES, source % LANES],
            send_sem=share_send.at[dest],
            recv_sem=share_recv.at[source],
            device_id=(z * LANES + dest % LANES, dest // LANES),
            device_id_type=MESH,
        )

    each(1, crowd, lambda step: share_copy(inside, (inside + step) % crowd).start())
    share_buf[tp_here, lane] = part_buf[tp_here, lane]
    each(1, crowd, lambda step: share_copy((inside + step) % crowd, inside).wait_recv())

    sums = []
    for source in range(LANES):
        add = share_buf[0, source].astype(jnp.float32)
        for group in range(1, GROUPS):
            add = add + share_buf[group, source].astype(jnp.float32)
        sums.append(add)
    for quarter in range(4):
        for half in range(2):
            projected = jnp.concatenate(
                [sums[half * 4 + i][:, quarter * 32:(quarter + 1) * 32] for i in range(4)], axis=1
            )
            columns = slice((quarter * 2 + half) * DH, (quarter * 2 + half + 1) * DH)
            encoded = residual_ref[:, columns].astype(jnp.float32) + gain_ref[:, columns] * projected
            encoded_ref[:, columns] = encoded.astype(encoded_ref.dtype)

    each(1, LANES, lambda step: stage_copy(lane, (lane + step) % LANES).wait_send())

    def ring_sent(step):
        ring_copy(plane_at(-step), 0, 0).wait_send()
        ring_copy(plane_at(step), 1, 1).wait_send()
        weight_copy(plane_at(-step), 0).wait_send()

        @pl.when(step < HALF_RING - 1)
        def _():
            ring_copy(plane_at(-step), 1, 0).wait_send()
            ring_copy(plane_at(step), 0, 1).wait_send()
            weight_copy(plane_at(step), 1).wait_send()

    each(0, HALF_RING, ring_sent)
    each(1, GROUPS, lambda step: plane_copy(lane, mate(step)).wait_send())
    each(0, GROUPS, lambda step: plane_copy(mate(step), sibling).wait_send())
    each(1, crowd, lambda step: share_copy(inside, (inside + step) % crowd).wait_send())


def local(
    query_states,
    key_states,
    value_states,
    residual,
    segment_ids,
    positions,
    out_weight,
    layer_scale,
):
    vmem = pl.BlockSpec(memory_space=pltpu.VMEM)
    columns, features = out_weight.shape[1], out_weight.shape[0]
    dma = pltpu.SemaphoreType.DMA
    return pl.pallas_call(
        layer_kernel,
        out_shape=jax.ShapeDtypeStruct(residual.shape, jnp.bfloat16),
        in_specs=[vmem] * 8,
        out_specs=vmem,
        scratch_shapes=[
            pltpu.VMEM((LANES, 3, SPAN, DH), jnp.bfloat16),
            pltpu.VMEM((LANES, 3, SPAN, DH), jnp.bfloat16),
            pltpu.VMEM((PLANES, 2, TOKENS, DH), jnp.bfloat16),
            pltpu.VMEM((PLANES, columns, features), jnp.bfloat16),
            pltpu.VMEM((TOKENS, CHUNK), jnp.float32),
            pltpu.VMEM((TOKENS, DH), jnp.float32),
            pltpu.VMEM((TOKENS, DH), jnp.float32),
            pltpu.VMEM((TOKENS, DH), jnp.float32),
            pltpu.VMEM((LANES, TOKENS, DH), jnp.bfloat16),
            pltpu.VMEM((GROUPS, LANES, SPAN, DH), jnp.bfloat16),
            pltpu.VMEM((GROUPS, LANES, SPAN, DH), jnp.bfloat16),
            dma((LANES,)),
            dma((LANES,)),
            dma((2, PLANES, 2)),
            dma((PLANES, 2)),
            dma((2, PLANES)),
            dma((PLANES,)),
            dma((LANES, LANES)),
            dma((LANES,)),
            dma((GROUPS * LANES,)),
            dma((GROUPS * LANES,)),
        ],
        compiler_params=pltpu.CompilerParams(
            collective_id=0, has_side_effects=True, vmem_limit_bytes=40 * 1024 * 1024
        ),
    )(
        query_states,
        key_states,
        value_states,
        residual,
        segment_ids.reshape(-1, CHUNK),
        positions.T,
        out_weight.T,
        layer_scale[None, :],
    )


def solution(mesh):
    in_specs = (
        P("seq", "tp"),
        P("seq", "tp"),
        P("seq", "tp"),
        P("seq", "tp"),
        P(),
        P(None, "seq"),
        P("tp", "seq"),
        P("tp"),
    )
    out_specs = P("seq", "tp")
    return jax.shard_map(local, mesh=mesh, in_specs=in_specs, out_specs=out_specs, check_vma=False)
```

time: 360 us -> 106 us (0.29)
  waiting for transfers between devices: 234 us -> 0 us
  Pallas kernels: 0 us -> 99.4 us
  starting transfers between devices: 38.2 us -> 0 us
  blocking collectives: 26.4 us -> 0 us
  matrix products: 24 us -> 0 us
  between operations: 13.6 us -> 0.03 us
  other arithmetic: 11.7 us -> 0 us
  local copies, waits for them, and re-layouts: 10.2 us -> 5.89 us
    all_to_all x3 -> x0, waiting for transfers between devices: 212 us -> none  [the longest x1 100 us: local(): lax.all_to_all(spread(rotated_k), 'seq', split_axis=0, concat_axis=1, til...]
    pallas_call x0 -> x1, Pallas kernels: none -> 99.4 us  [local(): pl.pallas_call(layer_kernel, out_shape=jax.ShapeDtypeStruct(residual.shap...]
    all_to_all x3 -> x0, starting transfers between devices: 37.9 us -> none  [the longest x1 20.6 us: local(): lax.all_to_all(query_send, 'seq', split_axis=0, concat_axis=1, tiled=True)]
    all_to_all x1 -> x0, blocking collectives: 26.4 us -> none  [local(): lax.all_to_all(attended, 'seq', split_axis=0, concat_axis=0, tiled=True)]
    dot_general x3 -> x0, matrix products: 24 us -> none  [the longest x1 8.83 us: attend_block(): jnp.dot(query_block, key_item.T, preferred_element_type=jnp.float32)]
    reduce_scatter x1 -> x0, waiting for transfers between devices: 20.8 us -> none  [local(): lax.psum_scatter(partial_value, 'tp', scatter_dimension=1, tiled=True)]
    reduce_sum x1 -> x0, other arithmetic: 8.16 us -> none  [attend_block(): row_total = jnp.sum(exponent, axis=1, keepdims=True)]
    broadcast_in_dim x2 -> x0, local copies, waits for them, and re-layouts: 3.85 us -> none  [spread(): jnp.broadcast_to(by_head[:, None], (head_count, query_parts, local_span,...]
  transfers between devices with their start and end apart: 5 -> 0, of which waited for: 4 -> 0; matrix products, arithmetic and copies ran while one was open for 8% -> 0% of each run, Pallas kernels for 0% -> 0%
where the time goes in v3:
time: 106 us; the launch traced here: 105 us
  Pallas kernels  99.4 us (94%)
  local copies, waits for them, and re-layouts  5.89 us (6%)
    pallas_call x1, Pallas kernels, local(): pl.pallas_call(layer_kernel, out_shape=jax.ShapeDtypeStruct(residual.shap...  99.4 us
    unnamed x16, local copies, waits for them, and re-layouts  5.89 us

profile of v3, /device:TPU:1, one launch (start us, length us, event | category | flops | bytes accessed | tf_op | source)
XLA Modules:
  0.0 105.3 jit_solution(3437131184892256111)
XLA Ops:
  0.0 0.0 copy-start.5
  0.0 0.0 copy-start.6
  0.0 0.8 copy.9
  0.8 0.0 copy-done.5
  0.8 0.0 copy-done.6
  0.8 0.0 copy-start
  0.8 0.9 copy-done
  1.7 0.0 copy-start.1
  1.7 0.9 copy-done.1
  2.6 0.0 copy-start.2
  2.6 0.9 copy-done.2
  3.5 0.0 copy-start.3
  3.5 0.9 copy-done.3
  4.4 0.0 copy-start.4
  4.4 0.8 copy-done.4
  5.2 99.4 %shard_map.82 = bf16[64,1024]{1,0:T(8,128)(2,1)S(1)} custom-call(bf16[64,1024]{1,0:T(8,128)(2,1)S(1)} %copy-done, bf16[64,1024]{1,0:T(8,128)(2,1)S(1)} %copy-done.1, bf16[64,1024]{1,0:T(8,128)(2,1)S(1)} %copy-done.2, bf16[64,1024]{1,0:T(8,128)(2,1)S(1)} %copy-done.3, s32[64,128]{1,0:T(8,128)S(1)} %bitcast.6, s32[64,2]{1,0:T(8,128)S(1)} %bitcast.4, ...), custom_call_target="tpu_custom_call" | custom-call | tf_op jit(solution)/shard_map/pallas_call | solution.py:365
  104.7 0.7 copy.11
Async XLA Ops:
  0.0 0.8 copy-start.5
  0.0 0.8 copy-start.6
  0.8 0.9 copy-start
  1.7 0.9 copy-start.1
  2.6 0.9 copy-start.2
  3.5 0.9 copy-start.3
  4.4 0.8 copy-start.4

commit v4 on v3

v4 whole, which is shorter than its diff:
```python
import math

import jax
import jax.numpy as jnp
from jax import lax
from jax.experimental import pallas as pl
from jax.experimental.pallas import tpu as pltpu
from jax.sharding import PartitionSpec as P

DH = 128
PLANES = 16
LANES = 8
GROUPS = 4
SPAN = 64
TOKENS = LANES * SPAN
CHUNK = 128
HALF_RING = PLANES // 2
PIECES = 4
PARTS = TOKENS // CHUNK
PER_PART = LANES // PARTS
EXPONENT_SCALE = DH ** (-0.5) * math.log2(math.e)
MESH = pl.DeviceIdType.MESH

masked_score = -1e30


def each(start, stop, act):
    def body(step, carry):
        act(step)
        return carry

    lax.fori_loop(start, stop, body, 0)


def layer_kernel(
    query_ref,
    key_ref,
    value_ref,
    residual_ref,
    segment_ref,
    position_ref,
    weight_ref,
    gain_ref,
    encoded_ref,
    query_buf,
    key_buf,
    value_buf,
    residual_buf,
    send_buf,
    stage_buf,
    kv_buf,
    weight_buf,
    query_segment,
    peak_ref,
    total_ref,
    sum_ref,
    plane_buf,
    part_buf,
    share_buf,
    stage_send,
    stage_recv,
    ring_send,
    ring_recv,
    weight_send,
    weight_recv,
    mate_send,
    sibling_send,
    plane_recv,
    share_send,
    share_recv,
    load_sem,
):
    seq_here, tp_here = lax.axis_index("seq"), lax.axis_index("tp")
    z, lane = seq_here // LANES, seq_here % LANES
    row, core = lane // 2, lane % 2
    inside = tp_here * LANES + lane
    crowd = GROUPS * LANES

    def plane_at(step):
        return (z + step + PLANES) % PLANES

    loads = [
        pltpu.make_async_copy(source, dest, load_sem.at[index])
        for index, (source, dest) in enumerate(
            [
                (query_ref, query_buf),
                (key_ref, key_buf),
                (value_ref, value_buf),
                (weight_ref, weight_buf.at[z]),
                (residual_ref, residual_buf),
            ]
        )
    ]
    for load in loads:
        load.start()

    up = (plane_at(1) * LANES + lane, tp_here)
    down = (plane_at(-1) * LANES + lane, tp_here)

    barrier = pltpu.get_barrier_semaphore()

    def greet(device):
        pl.semaphore_signal(barrier, inc=1, device_id=device, device_id_type=MESH)

    greet(up)
    greet(down)

    def greet_inside(step):
        other = (inside + step) % crowd
        greet((z * LANES + other % LANES, other // LANES))

    each(1, crowd, greet_inside)

    def weight_copy(plane, way):
        return pltpu.make_async_remote_copy(
            src_ref=weight_buf.at[plane],
            dst_ref=weight_buf.at[plane],
            send_sem=weight_send.at[way, plane],
            recv_sem=weight_recv.at[plane],
            device_id=up if way == 0 else down,
            device_id_type=MESH,
        )

    def ring_copy(plane, piece, way):
        return pltpu.make_async_remote_copy(
            src_ref=kv_buf.at[plane, piece],
            dst_ref=kv_buf.at[plane, piece],
            send_sem=ring_send.at[way, plane, piece],
            recv_sem=ring_recv.at[plane, piece],
            device_id=up if way == 0 else down,
            device_id_type=MESH,
        )

    def stage_copy(source, dest):
        return pltpu.make_async_remote_copy(
            src_ref=send_buf.at[dest],
            dst_ref=stage_buf.at[source],
            send_sem=stage_send.at[dest],
            recv_sem=stage_recv.at[source],
            device_id=(z * LANES + dest, tp_here),
            device_id_type=MESH,
        )

    def weight_hop(hop):
        weight_copy(plane_at(-hop), 0).wait_recv()
        weight_copy(plane_at(-hop), 0).start()
        weight_copy(plane_at(hop), 1).wait_recv()
        weight_copy(plane_at(hop), 1).start()

    lanes = lax.broadcasted_iota(jnp.int32, (SPAN, DH), 1)
    frequency = jnp.exp((lanes % 32).astype(jnp.float32) * (-math.log(100.0) / 32))
    grid_row, grid_column = [
        jnp.broadcast_to(position_ref[axis:axis + 1, :].astype(jnp.float32), (DH, SPAN)).T
        for axis in range(2)
    ]
    angle = jnp.where(lanes < DH // 2, grid_row, grid_column) * frequency
    first = lanes % 64 < 32
    cosine = jnp.cos(angle)
    sine = jnp.sin(angle)
    sine = jnp.where(first, -sine, sine)

    def rotate(states):
        states = states.astype(jnp.float32)
        partner = jnp.where(
            first, pltpu.roll(states, DH - 32, axis=1), pltpu.roll(states, 32, axis=1)
        )
        return (states * cosine + partner * sine).astype(jnp.bfloat16)

    for load in loads[:3]:
        load.wait()
    for head in range(LANES):
        features = slice(head * DH, (head + 1) * DH)
        send_buf[head, 0] = rotate(query_buf[:, features])
        send_buf[head, 1] = rotate(key_buf[:, features])
        send_buf[head, 2] = value_buf[:, features]
    loads[3].wait()

    pl.semaphore_wait(barrier, 2 + crowd - 1)
    weight_copy(z, 0).start()
    weight_copy(z, 1).start()
    each(1, LANES, lambda step: stage_copy(lane, (lane + step) % LANES).start())
    stage_buf[lane] = send_buf[lane]

    for part in range(PARTS):
        own = segment_ref[pl.ds(z * PARTS + part, 1), :].astype(jnp.float32)
        query_segment[part * CHUNK:(part + 1) * CHUNK] = jnp.broadcast_to(own, (CHUNK, CHUNK)).T
    peak_ref[...] = jnp.full(peak_ref.shape, masked_score, jnp.float32)
    total_ref[...] = jnp.zeros(total_ref.shape, jnp.float32)
    sum_ref[...] = jnp.zeros(sum_ref.shape, jnp.float32)

    def attend(plane, chunk):
        key = kv_buf[plane, 0:2].reshape(TOKENS, DH)
        value = kv_buf[plane, 2:4].reshape(TOKENS, DH)
        rows = slice(chunk * CHUNK, (chunk + 1) * CHUNK)
        query = stage_buf[chunk * PER_PART:(chunk + 1) * PER_PART, 0].reshape(CHUNK, DH)
        score = lax.dot_general(
            query, key, (((1,), (1,)), ((), ())), preferred_element_type=jnp.float32
        )
        segment = query_segment[rows]
        scores = [
            jnp.where(
                segment == segment_ref[pl.ds(plane * PARTS + part, 1), :].astype(jnp.float32),
                score[:, part * CHUNK:(part + 1) * CHUNK],
                masked_score,
            )
            for part in range(PARTS)
        ]
        top = jnp.maximum(
            jnp.maximum(scores[0], scores[1]), jnp.maximum(scores[2], scores[3])
        )
        old = peak_ref[rows]
        peak = jnp.maximum(old, jnp.max(top, axis=1, keepdims=True))
        peak_ref[rows] = peak
        fade = jnp.exp2((old - peak) * EXPONENT_SCALE)
        exponents = [jnp.exp2((part - peak) * EXPONENT_SCALE) for part in scores]
        total_ref[rows] = total_ref[rows] * fade + (
            (exponents[0] + exponents[1]) + (exponents[2] + exponents[3])
        )
        weights = jnp.concatenate([part.astype(jnp.bfloat16) for part in exponents], axis=1)
        sum_ref[rows] = sum_ref[rows] * fade + jnp.dot(
            weights, value, preferred_element_type=jnp.float32
        )

    weight_hop(1)
    weight_hop(2)

    each(1, LANES, lambda step: stage_copy((lane + step) % LANES, lane).wait_recv())
    for which in range(2):
        states = stage_buf[:, 1 + which].reshape(2, TOKENS // 2, DH)
        kv_buf[z, 2 * which:2 * which + 2] = states
    for piece in range(PIECES):
        ring_copy(z, piece, 0).start()
        ring_copy(z, piece, 1).start()
        attend(z, piece)

    def ring_step(step):
        below, above = plane_at(-step), plane_at(step)
        for piece in range(PIECES):
            keys = piece < PIECES // 2
            ring_copy(below, piece, 0).wait_recv()
            if keys:
                ring_copy(below, piece, 0).start()
            else:
                pl.when(step < HALF_RING - 1)(lambda: ring_copy(below, piece, 0).start())
            ring_copy(above, piece, 1).wait_recv()
            if keys:
                pl.when(step < HALF_RING - 1)(lambda: ring_copy(above, piece, 1).start())
            else:
                ring_copy(above, piece, 1).start()

            @pl.when(step > 1)
            def _():
                attend(plane_at(1 - step), piece)
                attend(plane_at(step - 1), piece)

        @pl.when(jnp.logical_and(step % 2 == 1, step < HALF_RING - 1))
        def _():
            weight_hop(3 + step // 2)

    each(1, HALF_RING, ring_step)
    far = plane_at(HALF_RING)
    for piece in range(PIECES):
        ring_copy(far, piece, 0 if piece < PIECES // 2 else 1).wait_recv()
        attend(plane_at(1 - HALF_RING), piece)
        attend(plane_at(HALF_RING - 1), piece)
    weight_hop(6)

    sibling = row * 2 + 1 - core

    def mate(step):
        return ((row + step) % GROUPS) * 2 + core

    def sibling_of(step):
        return ((row + step) % GROUPS) * 2 + 1 - core

    def plane_copy(slot, chunk, device_lane, send_sem):
        return pltpu.make_async_remote_copy(
            src_ref=plane_buf.at[slot, chunk],
            dst_ref=plane_buf.at[slot, chunk],
            send_sem=send_sem,
            recv_sem=plane_recv.at[slot, chunk],
            device_id=(z * LANES + device_lane, tp_here),
            device_id_type=MESH,
        )

    def to_mate(step, chunk):
        return plane_copy(lane, chunk, mate(step), mate_send.at[step, chunk])

    def to_sibling(step, chunk):
        return plane_copy(mate(step), chunk, sibling, sibling_send.at[step, chunk])

    def from_sibling(step, chunk):
        return plane_copy(sibling_of(step), chunk, lane, sibling_send.at[step, chunk])

    for chunk in range(PARTS):
        attend(far, chunk)
        rows = slice(chunk * CHUNK, (chunk + 1) * CHUNK)
        total = jnp.sum(total_ref[rows], axis=1, keepdims=True)
        plane_buf[lane, chunk] = (sum_ref[rows] / total).astype(jnp.bfloat16)
        each(1, GROUPS, lambda step: to_mate(step, chunk).start())
        to_sibling(0, chunk).start()

    weight_copy(plane_at(-7), 0).wait_recv()
    weight_copy(plane_at(-7), 0).start()
    weight_copy(plane_at(7), 1).wait_recv()

    def pass_on(chunk):
        def act(step):
            to_sibling(step, chunk).wait_recv()
            to_sibling(step, chunk).start()

        each(1, GROUPS, act)

    def share_copy(source, dest):
        return pltpu.make_async_remote_copy(
            src_ref=part_buf.at[dest // LANES, dest % LANES],
            dst_ref=share_buf.at[source // LANES, source % LANES],
            send_sem=share_send.at[dest],
            recv_sem=share_recv.at[source],
            device_id=(z * LANES + dest % LANES, dest // LANES),
            device_id_type=MESH,
        )

    pass_on(0)
    for chunk in range(PARTS):
        if chunk + 1 < PARTS:
            pass_on(chunk + 1)
        if chunk == 0:
            weight_copy(far, 0).wait_recv()
        each(0, GROUPS, lambda step: from_sibling(step, chunk).wait_recv())
        token = jnp.concatenate([plane_buf[head, chunk] for head in range(LANES)], axis=1)
        part = lax.dot_general(
            token,
            weight_buf[...].reshape(GROUPS * DH, LANES * DH),
            (((1,), (1,)), ((), ())),
            preferred_element_type=jnp.float32,
        ).astype(jnp.bfloat16)
        for group in range(GROUPS):
            part_buf[group, chunk * PER_PART:(chunk + 1) * PER_PART] = part[
                :, group * DH:(group + 1) * DH
            ].reshape(PER_PART, SPAN, DH)

        def share_out(step):
            dest = ((tp_here + step // PER_PART) % GROUPS) * LANES + chunk * PER_PART + step % PER_PART
            pl.when(dest != inside)(lambda: share_copy(inside, dest).start())

        each(0, GROUPS * PER_PART, share_out)

    share_buf[tp_here, lane] = part_buf[tp_here, lane]
    loads[4].wait()
    each(1, crowd, lambda step: share_copy((inside + step) % crowd, inside).wait_recv())

    sums = []
    for source in range(LANES):
        add = share_buf[0, source].astype(jnp.float32)
        for group in range(1, GROUPS):
            add = add + share_buf[group, source].astype(jnp.float32)
        sums.append(add)
    for quarter in range(4):
        for half in range(2):
            projected = jnp.concatenate(
                [sums[half * 4 + i][:, quarter * 32:(quarter + 1) * 32] for i in range(4)], axis=1
            )
            columns = slice((quarter * 2 + half) * DH, (quarter * 2 + half + 1) * DH)
            encoded = residual_buf[:, columns].astype(jnp.float32) + gain_ref[:, columns] * projected
            encoded_ref[:, columns] = encoded.astype(encoded_ref.dtype)

    each(1, LANES, lambda step: stage_copy(lane, (lane + step) % LANES).wait_send())

    def ring_sent(step):
        for piece in range(PIECES // 2):
            ring_copy(plane_at(-step), piece, 0).wait_send()
            ring_copy(plane_at(step), PIECES // 2 + piece, 1).wait_send()
        weight_copy(plane_at(-step), 0).wait_send()

        @pl.when(step < HALF_RING - 1)
        def _():
            for piece in range(PIECES // 2):
                ring_copy(plane_at(-step), PIECES // 2 + piece, 0).wait_send()
                ring_copy(plane_at(step), piece, 1).wait_send()
            weight_copy(plane_at(step), 1).wait_send()

    each(0, HALF_RING, ring_sent)

    def plane_sent(chunk):
        each(1, GROUPS, lambda step: to_mate(step, chunk).wait_send())
        each(0, GROUPS, lambda step: to_sibling(step, chunk).wait_send())

    each(0, PARTS, plane_sent)
    each(1, crowd, lambda step: share_copy(inside, (inside + step) % crowd).wait_send())


def local(
    query_states,
    key_states,
    value_states,
    residual,
    segment_ids,
    positions,
    out_weight,
    layer_scale,
):
    vmem = pl.BlockSpec(memory_space=pltpu.VMEM)
    hbm = pl.BlockSpec(memory_space=pltpu.HBM)
    columns, features = out_weight.shape[1], out_weight.shape[0]
    dma = pltpu.SemaphoreType.DMA
    return pl.pallas_call(
        layer_kernel,
        out_shape=jax.ShapeDtypeStruct(residual.shape, jnp.bfloat16),
        in_specs=[hbm, hbm, hbm, hbm, vmem, vmem, hbm, vmem],
        out_specs=vmem,
        scratch_shapes=[
            pltpu.VMEM(query_states.shape, jnp.bfloat16),
            pltpu.VMEM(query_states.shape, jnp.bfloat16),
            pltpu.VMEM(query_states.shape, jnp.bfloat16),
            pltpu.VMEM(query_states.shape, jnp.bfloat16),
            pltpu.VMEM((LANES, 3, SPAN, DH), jnp.bfloat16),
            pltpu.VMEM((LANES, 3, SPAN, DH), jnp.bfloat16),
            pltpu.VMEM((PLANES, PIECES, TOKENS // 2, DH), jnp.bfloat16),
            pltpu.VMEM((PLANES, columns, features), jnp.bfloat16),
            pltpu.VMEM((TOKENS, CHUNK), jnp.float32),
            pltpu.VMEM((TOKENS, DH), jnp.float32),
            pltpu.VMEM((TOKENS, DH), jnp.float32),
            pltpu.VMEM((TOKENS, DH), jnp.float32),
            pltpu.VMEM((LANES, PARTS, CHUNK, DH), jnp.bfloat16),
            pltpu.VMEM((GROUPS, LANES, SPAN, DH), jnp.bfloat16),
            pltpu.VMEM((GROUPS, LANES, SPAN, DH), jnp.bfloat16),
            dma((LANES,)),
            dma((LANES,)),
            dma((2, PLANES, PIECES)),
            dma((PLANES, PIECES)),
            dma((2, PLANES)),
            dma((PLANES,)),
            dma((GROUPS, PARTS)),
            dma((GROUPS, PARTS)),
            dma((LANES, PARTS)),
            dma((GROUPS * LANES,)),
            dma((GROUPS * LANES,)),
            dma((5,)),
        ],
        compiler_params=pltpu.CompilerParams(
            collective_id=0, has_side_effects=True, vmem_limit_bytes=56 * 1024 * 1024
        ),
    )(
        query_states,
        key_states,
        value_states,
        residual,
        segment_ids.reshape(-1, CHUNK),
        positions,
        out_weight.T,
        layer_scale[None, :],
    )


def solution(mesh):
    in_specs = (
        P("seq", "tp"),
        P("seq", "tp"),
        P("seq", "tp"),
        P("seq", "tp"),
        P(),
        P(None, "seq"),
        P("tp", "seq"),
        P("tp"),
    )
    out_specs = P("seq", "tp")
    return jax.shard_map(local, mesh=mesh, in_specs=in_specs, out_specs=out_specs, check_vma=False)
```

time: 106 us -> 98.3 us (0.927)
  Pallas kernels: 99.4 us -> 95 us
  local copies, waits for them, and re-layouts: 5.89 us -> 1.57 us
    pallas_call x1, Pallas kernels: 99.4 us -> 95 us  [local(): pl.pallas_call(layer_kernel, out_shape=jax.ShapeDtypeStruct(residual.shap...]
    unnamed x16 -> x1, local copies, waits for them, and re-layouts: 5.89 us -> 1.57 us
where the time goes in v4:
time: 98.3 us; the launch traced here: 96.6 us
  Pallas kernels  95 us (97%)
  local copies, waits for them, and re-layouts  1.57 us (2%)
    pallas_call x1, Pallas kernels, local(): pl.pallas_call(layer_kernel, out_shape=jax.ShapeDtypeStruct(residual.shap...  95 us

profile of v4, /device:TPU:1, one launch (start us, length us, event | category | flops | bytes accessed | tf_op | source)
XLA Modules:
  0.0 96.6 jit_solution(14626650543504024971)
XLA Ops:
  0.0 95.0 %shard_map.82 = bf16[64,1024]{1,0:T(8,128)(2,1)} custom-call(bf16[64,1024]{1,0:T(8,128)(2,1)} %query_ref.1, bf16[64,1024]{1,0:T(8,128)(2,1)} %key_ref.1, bf16[64,1024]{1,0:T(8,128)(2,1)} %value_ref.1, bf16[64,1024]{1,0:T(8,128)(2,1)} %residual_ref.1, s32[64,128]{1,0:T(8,128)} %bitcast.4, s32[2,64]{1,0:T(2,128)} %position_ref.1, bf16[32,1024]{1,0:T(8,128)(2,1)} %bitcast.3, ...), custom_call_target="tpu_custom_call" | custom-call | tf_op jit(solution)/shard_map/pallas_call | solution.py:407
  95.0 1.6 %copy.10 = bf16[64,1024]{1,0:T(8,128)(2,1)} copy(bf16[64,1024]{1,0:T(8,128)(2,1)} %shard_map.82) | data formatting | bytes 262144

commit v5 on v4

--- a/solution.py
+++ b/solution.py
@@ -16,8 +16,13 @@
 CHUNK = 128
 HALF_RING = PLANES // 2
 PIECES = 4
+KEYS = PIECES // 2
+SOURCES = LANES // KEYS
 PARTS = TOKENS // CHUNK
 PER_PART = LANES // PARTS
+TAIL = 4
+TAIL_ROWS = TOKENS // TAIL
+PER_TAIL = LANES // TAIL
 EXPONENT_SCALE = DH ** (-0.5) * math.log2(math.e)
 MESH = pl.DeviceIdType.MESH
 
@@ -63,8 +68,7 @@
     ring_recv,
     weight_send,
     weight_recv,
-    mate_send,
-    sibling_send,
+    plane_send,
     plane_recv,
     share_send,
     share_recv,
@@ -115,7 +119,7 @@
         return pltpu.make_async_remote_copy(
             src_ref=weight_buf.at[plane],
             dst_ref=weight_buf.at[plane],
-            send_sem=weight_send.at[way, plane],
+            send_sem=weight_send,
             recv_sem=weight_recv.at[plane],
             device_id=up if way == 0 else down,
             device_id_type=MESH,
@@ -125,21 +129,35 @@
         return pltpu.make_async_remote_copy(
             src_ref=kv_buf.at[plane, piece],
             dst_ref=kv_buf.at[plane, piece],
-            send_sem=ring_send.at[way, plane, piece],
+            send_sem=ring_send,
             recv_sem=ring_recv.at[plane, piece],
             device_id=up if way == 0 else down,
             device_id_type=MESH,
         )
 
-    def stage_copy(source, dest):
+    def landing(source, which):
+        if which == 0:
+            return stage_buf.at[source]
+        piece = (which - 1) * KEYS + source // SOURCES
+        start = pl.multiple_of(source % SOURCES * SPAN, SPAN)
+        return kv_buf.at[z, piece, pl.ds(start, SPAN)]
+
+    def stage_copy(source, dest, which):
         return pltpu.make_async_remote_copy(
-            src_ref=send_buf.at[dest],
-            dst_ref=stage_buf.at[source],
-            send_sem=stage_send.at[dest],
-            recv_sem=stage_recv.at[source],
+            src_ref=send_buf.at[which * LANES + dest],
+            dst_ref=landing(source, which),
+            send_sem=stage_send,
+            recv_sem=stage_recv.at[which, source],
             device_id=(z * LANES + dest, tp_here),
             device_id_type=MESH,
         )
+
+    def spread(which):
+        each(1, LANES, lambda step: stage_copy(lane, (lane + step) % LANES, which).start())
+        landing(lane, which)[...] = send_buf[which * LANES + lane]
+
+    def arrive(which):
+        each(1, LANES, lambda step: stage_copy((lane + step) % LANES, lane, which).wait_recv())
 
     def weight_hop(hop):
         weight_copy(plane_at(-hop), 0).wait_recv()
@@ -166,20 +184,23 @@
         )
         return (states * cosine + partner * sine).astype(jnp.bfloat16)
 
-    for load in loads[:3]:
-        load.wait()
+    loads[1].wait()
     for head in range(LANES):
-        features = slice(head * DH, (head + 1) * DH)
-        send_buf[head, 0] = rotate(query_buf[:, features])
-        send_buf[head, 1] = rotate(key_buf[:, features])
-        send_buf[head, 2] = value_buf[:, features]
+        send_buf[LANES + head] = rotate(key_buf[:, head * DH:(head + 1) * DH])
     loads[3].wait()
 
     pl.semaphore_wait(barrier, 2 + crowd - 1)
+    spread(1)
     weight_copy(z, 0).start()
     weight_copy(z, 1).start()
-    each(1, LANES, lambda step: stage_copy(lane, (lane + step) % LANES).start())
-    stage_buf[lane] = send_buf[lane]
+    loads[2].wait()
+    for head in range(LANES):
+        send_buf[2 * LANES + head] = value_buf[:, head * DH:(head + 1) * DH]
+    spread(2)
+    loads[0].wait()
+    for head in range(LANES):
+        send_buf[head] = rotate(query_buf[:, head * DH:(head + 1) * DH])
+    spread(0)
 
     for part in range(PARTS):
         own = segment_ref[pl.ds(z * PARTS + part, 1), :].astype(jnp.float32)
@@ -189,10 +210,10 @@
     sum_ref[...] = jnp.zeros(sum_ref.shape, jnp.float32)
 
     def attend(plane, chunk):
-        key = kv_buf[plane, 0:2].reshape(TOKENS, DH)
-        value = kv_buf[plane, 2:4].reshape(TOKENS, DH)
+        key = kv_buf[plane, :KEYS].reshape(TOKENS, DH)
+        value = kv_buf[plane, KEYS:].reshape(TOKENS, DH)
         rows = slice(chunk * CHUNK, (chunk + 1) * CHUNK)
-        query = stage_buf[chunk * PER_PART:(chunk + 1) * PER_PART, 0].reshape(CHUNK, DH)
+        query = stage_buf[chunk * PER_PART:(chunk + 1) * PER_PART].reshape(CHUNK, DH)
         score = lax.dot_general(
             query, key, (((1,), (1,)), ((), ())), preferred_element_type=jnp.float32
         )
@@ -221,49 +242,47 @@
             weights, value, preferred_element_type=jnp.float32
         )
 
-    weight_hop(1)
-    weight_hop(2)
-
-    each(1, LANES, lambda step: stage_copy((lane + step) % LANES, lane).wait_recv())
-    for which in range(2):
-        states = stage_buf[:, 1 + which].reshape(2, TOKENS // 2, DH)
-        kv_buf[z, 2 * which:2 * which + 2] = states
-    for piece in range(PIECES):
-        ring_copy(z, piece, 0).start()
-        ring_copy(z, piece, 1).start()
-        attend(z, piece)
+    for which in range(1, 3):
+        arrive(which)
+        for piece in range((which - 1) * KEYS, which * KEYS):
+            ring_copy(z, piece, 0).start()
+            ring_copy(z, piece, 1).start()
+        weight_hop(which)
+    arrive(0)
+    for chunk in range(PARTS):
+        attend(z, chunk)
+
+    def quarter(step, index):
+        attend(plane_at(-step if index < PARTS else step), index % PARTS)
+
+    def quarters(step, piece):
+        for index in range(piece * 2 * PARTS // PIECES, (piece + 1) * 2 * PARTS // PIECES):
+            quarter(step, index)
 
     def ring_step(step):
         below, above = plane_at(-step), plane_at(step)
         for piece in range(PIECES):
-            keys = piece < PIECES // 2
             ring_copy(below, piece, 0).wait_recv()
-            if keys:
+            if piece < KEYS:
                 ring_copy(below, piece, 0).start()
             else:
                 pl.when(step < HALF_RING - 1)(lambda: ring_copy(below, piece, 0).start())
             ring_copy(above, piece, 1).wait_recv()
-            if keys:
+            if piece < KEYS:
                 pl.when(step < HALF_RING - 1)(lambda: ring_copy(above, piece, 1).start())
             else:
                 ring_copy(above, piece, 1).start()
-
-            @pl.when(step > 1)
-            def _():
-                attend(plane_at(1 - step), piece)
-                attend(plane_at(step - 1), piece)
-
-        @pl.when(jnp.logical_and(step % 2 == 1, step < HALF_RING - 1))
-        def _():
-            weight_hop(3 + step // 2)
+            pl.when(step > 1)(lambda: quarters(step - 1, piece))
+        pl.when(step % 2 == 1)(lambda: weight_hop(3 + step // 2))
 
     each(1, HALF_RING, ring_step)
     far = plane_at(HALF_RING)
     for piece in range(PIECES):
-        ring_copy(far, piece, 0 if piece < PIECES // 2 else 1).wait_recv()
-        attend(plane_at(1 - HALF_RING), piece)
-        attend(plane_at(HALF_RING - 1), piece)
-    weight_hop(6)
+        ring_copy(far, piece, 0 if piece < KEYS else 1).wait_recv()
+        quarters(HALF_RING - 1, piece)
+    weight_copy(plane_at(-7), 0).wait_recv()
+    weight_copy(plane_at(-7), 0).start()
+    weight_copy(plane_at(7), 1).wait_recv()
 
     sibling = row * 2 + 1 - core
 
@@ -273,36 +292,33 @@
     def sibling_of(step):
         return ((row + step) % GROUPS) * 2 + 1 - core
 
-    def plane_copy(slot, chunk, device_lane, send_sem):
+    def plane_copy(slot, chunk, device_lane):
         return pltpu.make_async_remote_copy(
-            src_ref=plane_buf.at[slot, chunk],
-            dst_ref=plane_buf.at[slot, chunk],
-            send_sem=send_sem,
+            src_ref=plane_buf.at[slot * TAIL + chunk],
+            dst_ref=plane_buf.at[slot * TAIL + chunk],
+            send_sem=plane_send,
             recv_sem=plane_recv.at[slot, chunk],
             device_id=(z * LANES + device_lane, tp_here),
             device_id_type=MESH,
         )
 
     def to_mate(step, chunk):
-        return plane_copy(lane, chunk, mate(step), mate_send.at[step, chunk])
+        return plane_copy(lane, chunk, mate(step))
 
     def to_sibling(step, chunk):
-        return plane_copy(mate(step), chunk, sibling, sibling_send.at[step, chunk])
+        return plane_copy(mate(step), chunk, sibling)
 
     def from_sibling(step, chunk):
-        return plane_copy(sibling_of(step), chunk, lane, sibling_send.at[step, chunk])
-
-    for chunk in range(PARTS):
-        attend(far, chunk)
-        rows = slice(chunk * CHUNK, (chunk + 1) * CHUNK)
+        return plane_copy(sibling_of(step), chunk, lane)
+
+    for chunk in range(TAIL):
+        for quarter_index in range(chunk * PARTS // TAIL, (chunk + 1) * PARTS // TAIL):
+            attend(far, quarter_index)
+        rows = slice(chunk * TAIL_ROWS, (chunk + 1) * TAIL_ROWS)
         total = jnp.sum(total_ref[rows], axis=1, keepdims=True)
-        plane_buf[lane, chunk] = (sum_ref[rows] / total).astype(jnp.bfloat16)
+        plane_buf[lane * TAIL + chunk] = (sum_ref[rows] / total).astype(jnp.bfloat16)
         each(1, GROUPS, lambda step: to_mate(step, chunk).start())
         to_sibling(0, chunk).start()
-
-    weight_copy(plane_at(-7), 0).wait_recv()
-    weight_copy(plane_at(-7), 0).start()
-    weight_copy(plane_at(7), 1).wait_recv()
 
     def pass_on(chunk):
         def act(step):
@@ -313,22 +329,22 @@
 
     def share_copy(source, dest):
         return pltpu.make_async_remote_copy(
-            src_ref=part_buf.at[dest // LANES, dest % LANES],
-            dst_ref=share_buf.at[source // LANES, source % LANES],
-            send_sem=share_send.at[dest],
-            recv_sem=share_recv.at[source],
+            src_ref=part_buf.at[dest],
+            dst_ref=share_buf.at[source],
+            send_sem=share_send,
+            recv_sem=share_recv,
             device_id=(z * LANES + dest % LANES, dest // LANES),
             device_id_type=MESH,
         )
 
     pass_on(0)
-    for chunk in range(PARTS):
-        if chunk + 1 < PARTS:
+    for chunk in range(TAIL):
+        if chunk + 1 < TAIL:
             pass_on(chunk + 1)
         if chunk == 0:
             weight_copy(far, 0).wait_recv()
         each(0, GROUPS, lambda step: from_sibling(step, chunk).wait_recv())
-        token = jnp.concatenate([plane_buf[head, chunk] for head in range(LANES)], axis=1)
+        token = jnp.concatenate([plane_buf[head * TAIL + chunk] for head in range(LANES)], axis=1)
         part = lax.dot_general(
             token,
             weight_buf[...].reshape(GROUPS * DH, LANES * DH),
@@ -336,25 +352,35 @@
             preferred_element_type=jnp.float32,
         ).astype(jnp.bfloat16)
         for group in range(GROUPS):
-            part_buf[group, chunk * PER_PART:(chunk + 1) * PER_PART] = part[
+            start = group * LANES + chunk * PER_TAIL
+            part_buf[start:start + PER_TAIL] = part[
                 :, group * DH:(group + 1) * DH
-            ].reshape(PER_PART, SPAN, DH)
+            ].reshape(PER_TAIL, SPAN, DH)
 
         def share_out(step):
-            dest = ((tp_here + step // PER_PART) % GROUPS) * LANES + chunk * PER_PART + step % PER_PART
+            dest = ((tp_here + step // PER_TAIL) % GROUPS) * LANES + chunk * PER_TAIL + step % PER_TAIL
             pl.when(dest != inside)(lambda: share_copy(inside, dest).start())
 
-        each(0, GROUPS * PER_PART, share_out)
-
-    share_buf[tp_here, lane] = part_buf[tp_here, lane]
+        each(0, GROUPS * PER_TAIL, share_out)
+
+    own_share = pltpu.make_async_copy(part_buf.at[inside], share_buf.at[inside], share_recv)
+    own_share.start()
+
+    def drain(ref, sem):
+        pltpu.make_async_copy(ref, ref, sem).wait()
+
+    drain(send_buf.at[0:3 * (LANES - 1)], stage_send)
+    drain(kv_buf.at[0:PLANES - 1], ring_send)
+    drain(weight_buf.at[0:PLANES - 1], weight_send)
+    drain(plane_buf.at[0:TAIL * (LANES - 1)], plane_send)
     loads[4].wait()
-    each(1, crowd, lambda step: share_copy((inside + step) % crowd, inside).wait_recv())
+    drain(share_buf, share_recv)
 
     sums = []
     for source in range(LANES):
-        add = share_buf[0, source].astype(jnp.float32)
+        add = share_buf[source].astype(jnp.float32)
         for group in range(1, GROUPS):
-            add = add + share_buf[group, source].astype(jnp.float32)
+            add = add + share_buf[group * LANES + source].astype(jnp.float32)
         sums.append(add)
     for quarter in range(4):
         for half in range(2):
@@ -365,29 +391,7 @@
             encoded = residual_buf[:, columns].astype(jnp.float32) + gain_ref[:, columns] * projected
             encoded_ref[:, columns] = encoded.astype(encoded_ref.dtype)
 
-    each(1, LANES, lambda step: stage_copy(lane, (lane + step) % LANES).wait_send())
-
-    def ring_sent(step):
-        for piece in range(PIECES // 2):
-            ring_copy(plane_at(-step), piece, 0).wait_send()
-            ring_copy(plane_at(step), PIECES // 2 + piece, 1).wait_send()
-        weight_copy(plane_at(-step), 0).wait_send()
-
-        @pl.when(step < HALF_RING - 1)
-        def _():
-            for piece in range(PIECES // 2):
-                ring_copy(plane_at(-step), PIECES // 2 + piece, 0).wait_send()
-                ring_copy(plane_at(step), piece, 1).wait_send()
-            weight_copy(plane_at(step), 1).wait_send()
-
-    each(0, HALF_RING, ring_sent)
-
-    def plane_sent(chunk):
-        each(1, GROUPS, lambda step: to_mate(step, chunk).wait_send())
-        each(0, GROUPS, lambda step: to_sibling(step, chunk).wait_send())
-
-    each(0, PARTS, plane_sent)
-    each(1, crowd, lambda step: share_copy(inside, (inside + step) % crowd).wait_send())
+    drain(part_buf.at[0:crowd - 1], share_send)
 
 
 def local(
@@ -414,28 +418,27 @@
             pltpu.VMEM(query_states.shape, jnp.bfloat16),
             pltpu.VMEM(query_states.shape, jnp.bfloat16),
             pltpu.VMEM(query_states.shape, jnp.bfloat16),
-            pltpu.VMEM((LANES, 3, SPAN, DH), jnp.bfloat16),
-            pltpu.VMEM((LANES, 3, SPAN, DH), jnp.bfloat16),
-            pltpu.VMEM((PLANES, PIECES, TOKENS // 2, DH), jnp.bfloat16),
+            pltpu.VMEM((3 * LANES, SPAN, DH), jnp.bfloat16),
+            pltpu.VMEM((LANES, SPAN, DH), jnp.bfloat16),
+            pltpu.VMEM((PLANES, PIECES, TOKENS // KEYS, DH), jnp.bfloat16),
             pltpu.VMEM((PLANES, columns, features), jnp.bfloat16),
             pltpu.VMEM((TOKENS, CHUNK), jnp.float32),
             pltpu.VMEM((TOKENS, DH), jnp.float32),
             pltpu.VMEM((TOKENS, DH), jnp.float32),
             pltpu.VMEM((TOKENS, DH), jnp.float32),
-            pltpu.VMEM((LANES, PARTS, CHUNK, DH), jnp.bfloat16),
-            pltpu.VMEM((GROUPS, LANES, SPAN, DH), jnp.bfloat16),
-            pltpu.VMEM((GROUPS, LANES, SPAN, DH), jnp.bfloat16),
-            dma((LANES,)),
-            dma((LANES,)),
-            dma((2, PLANES, PIECES)),
+            pltpu.VMEM((LANES * TAIL, TAIL_ROWS, DH), jnp.bfloat16),
+            pltpu.VMEM((GROUPS * LANES, SPAN, DH), jnp.bfloat16),
+            pltpu.VMEM((GROUPS * LANES, SPAN, DH), jnp.bfloat16),
+            dma(()),
+            dma((3, LANES)),
+            dma(()),
             dma((PLANES, PIECES)),
-            dma((2, PLANES)),
+            dma(()),
             dma((PLANES,)),
-            dma((GROUPS, PARTS)),
-            dma((GROUPS, PARTS)),
-            dma((LANES, PARTS)),
-            dma((GROUPS * LANES,)),
-            dma((GROUPS * LANES,)),
+            dma(()),
+            dma((LANES, TAIL)),
+            dma(()),
+            dma(()),
             dma((5,)),
         ],
         compiler_params=pltpu.CompilerParams(

time: 98.3 us -> 94.7 us (0.963); the launches traced: 96.6 us -> 94.5 us
  Pallas kernels: 95 us -> 92.9 us
    pallas_call x1, Pallas kernels: 95 us -> 92.9 us  [local(): pl.pallas_call(layer_kernel, out_shape=jax.ShapeDtypeStruct(residual.shap...]
where the time goes in v5:
time: 94.7 us; the launch traced here: 94.5 us
  Pallas kernels  92.9 us (98%)
  local copies, waits for them, and re-layouts  1.57 us (2%)
    pallas_call x1, Pallas kernels, local(): pl.pallas_call(layer_kernel, out_shape=jax.ShapeDtypeStruct(residual.shap...  92.9 us

profile of v5, /device:TPU:1, one launch (start us, length us, event | category | flops | bytes accessed | tf_op | source)
XLA Modules:
  0.0 94.5 jit_solution(14067622849692854843)
XLA Ops:
  0.0 92.9 %shard_map.82 = bf16[64,1024]{1,0:T(8,128)(2,1)} custom-call(bf16[64,1024]{1,0:T(8,128)(2,1)} %query_ref.1, bf16[64,1024]{1,0:T(8,128)(2,1)} %key_ref.1, bf16[64,1024]{1,0:T(8,128)(2,1)} %value_ref.1, bf16[64,1024]{1,0:T(8,128)(2,1)} %residual_ref.1, s32[64,128]{1,0:T(8,128)} %bitcast.4, s32[2,64]{1,0:T(2,128)} %position_ref.1, bf16[32,1024]{1,0:T(8,128)(2,1)} %bitcast.3, ...), custom_call_target="tpu_custom_call" | custom-call | tf_op jit(solution)/shard_map/pallas_call | solution.py:411
  92.9 1.6 %copy.10 = bf16[64,1024]{1,0:T(8,128)(2,1)} copy(bf16[64,1024]{1,0:T(8,128)(2,1)} %shard_map.82) | data formatting | bytes 262144

commit v6 on v5

--- a/solution.py
+++ b/solution.py
@@ -147,17 +147,20 @@
             src_ref=send_buf.at[which * LANES + dest],
             dst_ref=landing(source, which),
             send_sem=stage_send,
-            recv_sem=stage_recv.at[which, source],
+            recv_sem=stage_recv.at[which],
             device_id=(z * LANES + dest, tp_here),
             device_id_type=MESH,
         )
 
     def spread(which):
         each(1, LANES, lambda step: stage_copy(lane, (lane + step) % LANES, which).start())
-        landing(lane, which)[...] = send_buf[which * LANES + lane]
+        pltpu.make_async_copy(
+            send_buf.at[which * LANES + lane], landing(lane, which), stage_recv.at[which]
+        ).start()
 
     def arrive(which):
-        each(1, LANES, lambda step: stage_copy((lane + step) % LANES, lane, which).wait_recv())
+        whole = stage_buf if which == 0 else kv_buf.at[z, (which - 1) * KEYS:which * KEYS]
+        pltpu.make_async_copy(whole, whole, stage_recv.at[which]).wait()
 
     def weight_hop(hop):
         weight_copy(plane_at(-hop), 0).wait_recv()
@@ -410,7 +413,7 @@
     dma = pltpu.SemaphoreType.DMA
     return pl.pallas_call(
         layer_kernel,
-        out_shape=jax.ShapeDtypeStruct(residual.shape, jnp.bfloat16),
+        out_shape=pltpu.VMEM(residual.shape, jnp.bfloat16),
         in_specs=[hbm, hbm, hbm, hbm, vmem, vmem, hbm, vmem],
         out_specs=vmem,
         scratch_shapes=[
@@ -430,7 +433,7 @@
             pltpu.VMEM((GROUPS * LANES, SPAN, DH), jnp.bfloat16),
             pltpu.VMEM((GROUPS * LANES, SPAN, DH), jnp.bfloat16),
             dma(()),
-            dma((3, LANES)),
+            dma((3,)),
             dma(()),
             dma((PLANES, PIECES)),
             dma(()),

time: 94.7 us -> 93 us (0.982)
  no operation moved by 1% of the time
where the time goes in v6:
time: 93 us; the launch traced here: 92.8 us
  Pallas kernels  92.1 us (99%)
    pallas_call x1, Pallas kernels, local(): pl.pallas_call(layer_kernel, out_shape=pltpu.VMEM(residual.shape, jnp.bfl...  92.1 us

profile of v6, /device:TPU:1, one launch (start us, length us, event | category | flops | bytes accessed | tf_op | source)
XLA Modules:
  0.0 92.8 jit_solution(7697424902750651361)
XLA Ops:
  0.0 92.1 %shard_map.82 = bf16[64,1024]{1,0:T(8,128)(2,1)S(1)} custom-call(bf16[64,1024]{1,0:T(8,128)(2,1)} %query_ref.1, bf16[64,1024]{1,0:T(8,128)(2,1)} %key_ref.1, bf16[64,1024]{1,0:T(8,128)(2,1)} %value_ref.1, bf16[64,1024]{1,0:T(8,128)(2,1)} %residual_ref.1, s32[64,128]{1,0:T(8,128)} %bitcast.4, s32[2,64]{1,0:T(2,128)} %position_ref.1, ...), custom_call_target="tpu_custom_call" | custom-call | tf_op jit(solution)/shard_map/pallas_call | solution.py:414
  92.1 0.7 copy.10

commit v7 on v6

--- a/solution.py
+++ b/solution.py
@@ -16,8 +16,8 @@
 CHUNK = 128
 HALF_RING = PLANES // 2
 PIECES = 4
-KEYS = PIECES // 2
-SOURCES = LANES // KEYS
+HALF_PIECES = PIECES // 2
+SOURCES = LANES // HALF_PIECES
 PARTS = TOKENS // CHUNK
 PER_PART = LANES // PARTS
 TAIL = 4
@@ -70,9 +70,11 @@
     weight_recv,
     plane_send,
     plane_recv,
+    sibling_recv,
     share_send,
     share_recv,
     load_sem,
+    peer_sem,
 ):
     seq_here, tp_here = lax.axis_index("seq"), lax.axis_index("tp")
     z, lane = seq_here // LANES, seq_here % LANES
@@ -95,8 +97,8 @@
             ]
         )
     ]
-    for load in loads:
-        load.start()
+    for index in (2, 3, 1, 0, 4):
+        loads[index].start()
 
     up = (plane_at(1) * LANES + lane, tp_here)
     down = (plane_at(-1) * LANES + lane, tp_here)
@@ -109,11 +111,11 @@
     greet(up)
     greet(down)
 
-    def greet_inside(step):
-        other = (inside + step) % crowd
-        greet((z * LANES + other % LANES, other // LANES))
-
-    each(1, crowd, greet_inside)
+    def peer(step):
+        return (seq_here, (tp_here + step) % GROUPS)
+
+    each(1, LANES, lambda step: greet((z * LANES + (lane + step) % LANES, tp_here)))
+    each(1, GROUPS, lambda step: greet(peer(step)))
 
     def weight_copy(plane, way):
         return pltpu.make_async_remote_copy(
@@ -138,7 +140,7 @@
     def landing(source, which):
         if which == 0:
             return stage_buf.at[source]
-        piece = (which - 1) * KEYS + source // SOURCES
+        piece = (which - 1) * HALF_PIECES + source // SOURCES
         start = pl.multiple_of(source % SOURCES * SPAN, SPAN)
         return kv_buf.at[z, piece, pl.ds(start, SPAN)]
 
@@ -159,7 +161,7 @@
         ).start()
 
     def arrive(which):
-        whole = stage_buf if which == 0 else kv_buf.at[z, (which - 1) * KEYS:which * KEYS]
+        whole = stage_buf if which == 0 else kv_buf.at[z, (which - 1) * HALF_PIECES:which * HALF_PIECES]
         pltpu.make_async_copy(whole, whole, stage_recv.at[which]).wait()
 
     def weight_hop(hop):
@@ -167,6 +169,21 @@
         weight_copy(plane_at(-hop), 0).start()
         weight_copy(plane_at(hop), 1).wait_recv()
         weight_copy(plane_at(hop), 1).start()
+
+    loads[2].wait()
+    for head in range(LANES):
+        send_buf[LANES + head] = value_buf[:, head * DH:(head + 1) * DH]
+    loads[3].wait()
+
+    pl.semaphore_wait(barrier, 2 + LANES - 1 + GROUPS - 1)
+    spread(1)
+    weight_copy(z, 0).start()
+    weight_copy(z, 1).start()
+
+    def vouch(step):
+        pl.semaphore_signal(peer_sem, inc=1, device_id=peer(step), device_id_type=MESH)
+
+    each(1, GROUPS, vouch)
 
     lanes = lax.broadcasted_iota(jnp.int32, (SPAN, DH), 1)
     frequency = jnp.exp((lanes % 32).astype(jnp.float32) * (-math.log(100.0) / 32))
@@ -189,16 +206,7 @@
 
     loads[1].wait()
     for head in range(LANES):
-        send_buf[LANES + head] = rotate(key_buf[:, head * DH:(head + 1) * DH])
-    loads[3].wait()
-
-    pl.semaphore_wait(barrier, 2 + crowd - 1)
-    spread(1)
-    weight_copy(z, 0).start()
-    weight_copy(z, 1).start()
-    loads[2].wait()
-    for head in range(LANES):
-        send_buf[2 * LANES + head] = value_buf[:, head * DH:(head + 1) * DH]
+        send_buf[2 * LANES + head] = rotate(key_buf[:, head * DH:(head + 1) * DH])
     spread(2)
     loads[0].wait()
     for head in range(LANES):
@@ -213,8 +221,8 @@
     sum_ref[...] = jnp.zeros(sum_ref.shape, jnp.float32)
 
     def attend(plane, chunk):
-        key = kv_buf[plane, :KEYS].reshape(TOKENS, DH)
-        value = kv_buf[plane, KEYS:].reshape(TOKENS, DH)
+        value = kv_buf[plane, :HALF_PIECES].reshape(TOKENS, DH)
+        key = kv_buf[plane, HALF_PIECES:].reshape(TOKENS, DH)
         rows = slice(chunk * CHUNK, (chunk + 1) * CHUNK)
         query = stage_buf[chunk * PER_PART:(chunk + 1) * PER_PART].reshape(CHUNK, DH)
         score = lax.dot_general(
@@ -247,10 +255,10 @@
 
     for which in range(1, 3):
         arrive(which)
-        for piece in range((which - 1) * KEYS, which * KEYS):
+        for piece in range((which - 1) * HALF_PIECES, which * HALF_PIECES):
             ring_copy(z, piece, 0).start()
             ring_copy(z, piece, 1).start()
-        weight_hop(which)
+    weight_hop(1)
     arrive(0)
     for chunk in range(PARTS):
         attend(z, chunk)
@@ -266,22 +274,22 @@
         below, above = plane_at(-step), plane_at(step)
         for piece in range(PIECES):
             ring_copy(below, piece, 0).wait_recv()
-            if piece < KEYS:
+            if piece < HALF_PIECES:
                 ring_copy(below, piece, 0).start()
             else:
                 pl.when(step < HALF_RING - 1)(lambda: ring_copy(below, piece, 0).start())
             ring_copy(above, piece, 1).wait_recv()
-            if piece < KEYS:
+            if piece < HALF_PIECES:
                 pl.when(step < HALF_RING - 1)(lambda: ring_copy(above, piece, 1).start())
             else:
                 ring_copy(above, piece, 1).start()
             pl.when(step > 1)(lambda: quarters(step - 1, piece))
-        pl.when(step % 2 == 1)(lambda: weight_hop(3 + step // 2))
+        pl.when(step % 3 != 0)(lambda: weight_hop(step + 1 - step // 3))
 
     each(1, HALF_RING, ring_step)
     far = plane_at(HALF_RING)
     for piece in range(PIECES):
-        ring_copy(far, piece, 0 if piece < KEYS else 1).wait_recv()
+        ring_copy(far, piece, 0 if piece < HALF_PIECES else 1).wait_recv()
         quarters(HALF_RING - 1, piece)
     weight_copy(plane_at(-7), 0).wait_recv()
     weight_copy(plane_at(-7), 0).start()
@@ -292,27 +300,24 @@
     def mate(step):
         return ((row + step) % GROUPS) * 2 + core
 
-    def sibling_of(step):
-        return ((row + step) % GROUPS) * 2 + 1 - core
-
-    def plane_copy(slot, chunk, device_lane):
+    def plane_copy(slot, chunk, device_lane, recv_sem):
         return pltpu.make_async_remote_copy(
             src_ref=plane_buf.at[slot * TAIL + chunk],
             dst_ref=plane_buf.at[slot * TAIL + chunk],
             send_sem=plane_send,
-            recv_sem=plane_recv.at[slot, chunk],
+            recv_sem=recv_sem,
             device_id=(z * LANES + device_lane, tp_here),
             device_id_type=MESH,
         )
 
     def to_mate(step, chunk):
-        return plane_copy(lane, chunk, mate(step))
+        return plane_copy(lane, chunk, mate(step), plane_recv.at[row, chunk])
 
     def to_sibling(step, chunk):
-        return plane_copy(mate(step), chunk, sibling)
-
-    def from_sibling(step, chunk):
-        return plane_copy(sibling_of(step), chunk, lane)
+        return plane_copy(mate(step), chunk, sibling, sibling_recv.at[chunk])
+
+    def from_mate(step, chunk):
+        return plane_copy(mate(step), chunk, lane, plane_recv.at[(row + step) % GROUPS, chunk])
 
     for chunk in range(TAIL):
         for quarter_index in range(chunk * PARTS // TAIL, (chunk + 1) * PARTS // TAIL):
@@ -325,7 +330,7 @@
 
     def pass_on(chunk):
         def act(step):
-            to_sibling(step, chunk).wait_recv()
+            from_mate(step, chunk).wait_recv()
             to_sibling(step, chunk).start()
 
         each(1, GROUPS, act)
@@ -340,13 +345,17 @@
             device_id_type=MESH,
         )
 
+    pl.semaphore_wait(peer_sem, GROUPS - 1)
+    def drain(ref, sem):
+        pltpu.make_async_copy(ref, ref, sem).wait()
+
     pass_on(0)
     for chunk in range(TAIL):
         if chunk + 1 < TAIL:
             pass_on(chunk + 1)
         if chunk == 0:
             weight_copy(far, 0).wait_recv()
-        each(0, GROUPS, lambda step: from_sibling(step, chunk).wait_recv())
+        drain(plane_buf.at[0:GROUPS], sibling_recv.at[chunk])
         token = jnp.concatenate([plane_buf[head * TAIL + chunk] for head in range(LANES)], axis=1)
         part = lax.dot_general(
             token,
@@ -368,9 +377,6 @@
 
     own_share = pltpu.make_async_copy(part_buf.at[inside], share_buf.at[inside], share_recv)
     own_share.start()
-
-    def drain(ref, sem):
-        pltpu.make_async_copy(ref, ref, sem).wait()
 
     drain(send_buf.at[0:3 * (LANES - 1)], stage_send)
     drain(kv_buf.at[0:PLANES - 1], ring_send)
@@ -423,7 +429,7 @@
             pltpu.VMEM(query_states.shape, jnp.bfloat16),
             pltpu.VMEM((3 * LANES, SPAN, DH), jnp.bfloat16),
             pltpu.VMEM((LANES, SPAN, DH), jnp.bfloat16),
-            pltpu.VMEM((PLANES, PIECES, TOKENS // KEYS, DH), jnp.bfloat16),
+            pltpu.VMEM((PLANES, PIECES, TOKENS // HALF_PIECES, DH), jnp.bfloat16),
             pltpu.VMEM((PLANES, columns, features), jnp.bfloat16),
             pltpu.VMEM((TOKENS, CHUNK), jnp.float32),
             pltpu.VMEM((TOKENS, DH), jnp.float32),
@@ -439,10 +445,12 @@
             dma(()),
             dma((PLANES,)),
             dma(()),
-            dma((LANES, TAIL)),
+            dma((GROUPS, TAIL)),
+            dma((TAIL,)),
             dma(()),
             dma(()),
             dma((5,)),
+            pltpu.SemaphoreType.REGULAR,
         ],
         compiler_params=pltpu.CompilerParams(
             collective_id=0, has_side_effects=True, vmem_limit_bytes=56 * 1024 * 1024

time: 93 us -> 92.5 us (level)
  no operation moved by 1% of the time
where the time goes in v7:
time: 92.5 us; the launch traced here: 92.3 us
  Pallas kernels  91.6 us (99%)
    pallas_call x1, Pallas kernels, local(): pl.pallas_call(layer_kernel, out_shape=pltpu.VMEM(residual.shape, jnp.bfl...  91.6 us

profile of v7, /device:TPU:1, one launch (start us, length us, event | category | flops | bytes accessed | tf_op | source)
XLA Modules:
  0.0 92.3 jit_solution(9938041758998521736)
XLA Ops:
  0.0 91.6 %shard_map.82 = bf16[64,1024]{1,0:T(8,128)(2,1)S(1)} custom-call(bf16[64,1024]{1,0:T(8,128)(2,1)} %query_ref.1, bf16[64,1024]{1,0:T(8,128)(2,1)} %key_ref.1, bf16[64,1024]{1,0:T(8,128)(2,1)} %value_ref.1, bf16[64,1024]{1,0:T(8,128)(2,1)} %residual_ref.1, s32[64,128]{1,0:T(8,128)} %bitcast.4, s32[2,64]{1,0:T(2,128)} %position_ref.1, ...), custom_call_target="tpu_custom_call" | custom-call | tf_op jit(solution)/shard_map/pallas_call | solution.py:420
  91.6 0.7 copy.10

commit v8 on v7

--- a/solution.py
+++ b/solution.py
@@ -15,7 +15,7 @@
 TOKENS = LANES * SPAN
 CHUNK = 128
 HALF_RING = PLANES // 2
-PIECES = 4
+PIECES = 2
 HALF_PIECES = PIECES // 2
 SOURCES = LANES // HALF_PIECES
 PARTS = TOKENS // CHUNK

time: 92.5 us -> 91.1 us (0.985)
  Pallas kernels: 91.6 us -> 89.8 us
    pallas_call x1, Pallas kernels: 91.6 us -> 89.8 us  [local(): pl.pallas_call(layer_kernel, out_shape=pltpu.VMEM(residual.shape, jnp.bfl...]
where the time goes in v8:
time: 91.1 us; the launch traced here: 90.5 us
  Pallas kernels  89.8 us (99%)
    pallas_call x1, Pallas kernels, local(): pl.pallas_call(layer_kernel, out_shape=pltpu.VMEM(residual.shape, jnp.bfl...  89.8 us

profile of v8, /device:TPU:1, one launch (start us, length us, event | category | flops | bytes accessed | tf_op | source)
XLA Modules:
  0.0 90.5 jit_solution(12185592162463581650)
XLA Ops:
  0.0 89.8 %shard_map.82 = bf16[64,1024]{1,0:T(8,128)(2,1)S(1)} custom-call(bf16[64,1024]{1,0:T(8,128)(2,1)} %query_ref.1, bf16[64,1024]{1,0:T(8,128)(2,1)} %key_ref.1, bf16[64,1024]{1,0:T(8,128)(2,1)} %value_ref.1, bf16[64,1024]{1,0:T(8,128)(2,1)} %residual_ref.1, s32[64,128]{1,0:T(8,128)} %bitcast.4, s32[2,64]{1,0:T(2,128)} %position_ref.1, ...), custom_call_target="tpu_custom_call" | custom-call | tf_op jit(solution)/shard_map/pallas_call | solution.py:420
  89.8 0.7 copy.10
